TPU v7x, 256 devices: a whole 4x4x8 slice. The times are simulated.
256 devices in a mesh: train: 64 (over y, z, core), tile: 4 (over x).
Axes of the slice: x: 4, y: 4, z: 8, core: 2. Of those that a mesh axis runs over, the one named last changes fastest.
Arguments:
- test_grads: bfloat16 [8192, 4096], P('train', 'tile'), may hold values from -6 to 6
- fisher: bfloat16 [8, 512, 512], P('tile'), may hold values from -8 to 8
- train_grads: bfloat16 [262144, 4096], P(('train', 'tile')), may hold values from -0.09375 to 0.09375
- candidates: int32 [8192, 4], P('train'), may hold values from 0 to 63, all different within a row; in each aligned block of 128 rows (0 to 127, 128 to 255, ...) at most 12 rows name the same one
- shard_rows: int32 [64], P('train'), may hold values from 1024 to 4096
Outputs:
- top_scores: float32 [8192, 32], P('train')
Inputs may be any that keep to these rules, and one draw needn't show every extreme that they name: `candidates`: each row names 4 different shards; among the rows of one index of train no shard is named by more than 12 rows.
All inputs are finite; a program needn't handle non-finite values.
Results may differ from a plain program's by a relative error of at most 0.0011.
Values may be sent and summed in bfloat16 or wider, within the bound.
No kernel may reach another device: no remote copies, remote signals or barrier semaphores. Data moves between devices by JAX's collectives and lax.ppermute only.
A program may use at most 128 MiB of HBM per device.

v0:
```python
import functools

import jax
import jax.numpy as jnp
from jax import lax
from jax.experimental import pallas as pl
from jax.experimental.pallas import tpu as pltpu
from jax.sharding import PartitionSpec as P

TOPK = 32
LOWEST = -1.0e30
LANES = 128
SUBLANES = 8
ROW_BLOCK = TOPK * SUBLANES
WIDE, NARROW = 8, 4
VMEM_LIMIT = 56 * 1024 * 1024

f32, bf16, i32 = jnp.float32, jnp.bfloat16, jnp.int32


def iota(shape, dim):
    return lax.broadcasted_iota(i32, shape, dim)


def dot(a, b, dims=((1,), (0,))):
    return lax.dot_general(a, b, (dims, ((), ())), preferred_element_type=f32)


def sorting_pairs(n):
    pairs, p = [], 1
    while p < n:
        k = p
        while k >= 1:
            for j in range(k % p, n - k, 2 * k):
                for i in range(min(k, n - j - k)):
                    if (i + j) // (2 * p) == (i + j + k) // (2 * p):
                        pairs.append((i + j, i + j + k))
            k //= 2
        p *= 2
    return pairs


def exchange(v, i, j):
    v[i], v[j] = jnp.maximum(v[i], v[j]), jnp.minimum(v[i], v[j])


def sorted_down(v):
    v = list(v)
    for i, j in sorting_pairs(len(v)):
        exchange(v, i, j)
    return v


def bitonic_down(v):
    v, d = list(v), len(v) // 2
    while d:
        for i in range(len(v)):
            if not i & d:
                exchange(v, i, i + d)
        d //= 2
    return v


def best_of(a, b):
    return bitonic_down([jnp.maximum(x, y) for x, y in zip(a, reversed(b))])


def bitonic_rows(x, down):
    v = [x[i : i + SUBLANES] for i in range(0, TOPK, SUBLANES)]
    row = iota((SUBLANES, LANES), 0)
    for d in (2, 1):
        for i in range(len(v)):
            if not i & d:
                high, low = jnp.maximum(v[i], v[i + d]), jnp.minimum(v[i], v[i + d])
                v[i], v[i + d] = (high, low) if down else (low, high)
    for d in (4, 2, 1):
        first = (row & d) == 0
        for i, y in enumerate(v):
            after, before = pltpu.roll(y, SUBLANES - d, 0), pltpu.roll(y, d, 0)
            if down:
                v[i] = jnp.where(first, jnp.maximum(y, after), jnp.minimum(y, before))
            else:
                v[i] = jnp.where(first, jnp.minimum(y, after), jnp.maximum(y, before))
    return jnp.concatenate(v, axis=0)


def dispatch_kernel(grads_ref, fisher_ref, cand_ref, first_ref, second_ref, rank_ref):
    q_rows = grads_ref.shape[0]
    blocks, order, _ = fisher_ref.shape
    shards_n = first_ref.shape[0] // WIDE
    precond = jnp.concatenate(
        [
            dot(grads_ref[:, b * order : (b + 1) * order], fisher_ref[b]).astype(bf16)
            for b in range(blocks)
        ],
        axis=1,
    )
    half = blocks * order // 2
    cand = cand_ref[...]
    shard = iota((shards_n, q_rows), 0)
    naming = [cand[c : c + 1, :] == shard for c in range(cand.shape[0])]
    named = functools.reduce(jnp.logical_or, naming)
    before = (iota((q_rows, q_rows), 0) < iota((q_rows, q_rows), 1)).astype(f32).astype(bf16)
    rank = dot(named.astype(f32).astype(bf16), before)
    for c, here in enumerate(naming):
        at = jnp.sum(jnp.where(here, rank, 0.0), axis=0, keepdims=True)
        rank_ref[c : c + 1, :] = at.astype(i32)
    table = jnp.where(named, rank, 255.0).astype(bf16)
    rows = shards_n * WIDE
    spread = (iota((rows, shards_n), 0) // WIDE == iota((rows, shards_n), 1)).astype(f32)
    place = dot(spread.astype(bf16), table)
    row = iota((rows, q_rows), 0)
    pick = (place == (row % WIDE).astype(f32)).astype(f32).astype(bf16)
    first_ref[...] = dot(pick, precond).astype(bf16)
    pick = (place == (row % NARROW + WIDE).astype(f32)).astype(f32).astype(bf16)
    both = dot(pick, precond)
    upper = iota((rows, half), 0) // NARROW % 2 == 0
    second_ref[...] = jnp.where(upper, both[:, :half], both[:, half:]).astype(bf16)


def unfold_kernel(folded_ref, rows_ref):
    half = folded_ref.shape[1]
    upper = iota((SUBLANES, half), 0) < NARROW
    for i in range(0, rows_ref.shape[0], 2 * SUBLANES):
        x = folded_ref[2 * i : 2 * i + 4 * SUBLANES, :].astype(f32)
        built = []
        for k in (0, 2):
            a = x[k * SUBLANES : (k + 1) * SUBLANES]
            b = x[(k + 1) * SUBLANES : (k + 2) * SUBLANES]
            left = jnp.where(upper, a, pltpu.roll(b, NARROW, 0))
            right = jnp.where(upper, pltpu.roll(a, NARROW, 0), b)
            built.append(jnp.concatenate([left, right], axis=1))
        rows_ref[i : i + 2 * SUBLANES, :] = jnp.concatenate(built, axis=0).astype(bf16)


def score_kernel(slots, meta_ref, train_ref, *refs):
    q_refs, (out_ref, sum_ref, top_ref, turned_ref) = refs[:-4], refs[-4:]
    step = pl.program_id(0)
    me, live = meta_ref[0], meta_ref[1]
    width = train_ref.shape[1] // 4
    groups = sum_ref.shape[1] // LANES
    sources = out_ref.shape[0]

    @pl.when(step == 0)
    def _():
        top_ref[...] = jnp.full(top_ref.shape, LOWEST, f32)

    for j, pair in enumerate(q_refs[i : i + 2] for i in range(0, 8, 2)):
        away = (0, 3, 1, 2)[j]
        column = pl.multiple_of(((me + away) & 3) * width, width)
        q = jnp.concatenate([ref[...] for ref in pair], axis=0)
        part = dot(train_ref[:, pl.ds(column, width)], q, ((1,), (1,)))
        sum_ref[...] = part if j == 0 else sum_ref[...] + part

    row = iota((SUBLANES, LANES), 0) + step * ROW_BLOCK

    def group(g, carry):
        lanes = pl.ds(pl.multiple_of(g * LANES, LANES), LANES)
        v = []
        for k in range(TOPK):
            x = sum_ref[k * SUBLANES : (k + 1) * SUBLANES, lanes]
            v.append(jnp.where(row + k * SUBLANES < live, x, LOWEST))
        v = sorted_down(v)
        v = best_of(v, [top_ref[g, k] for k in range(TOPK)])
        for k in range(TOPK):
            top_ref[g, k] = v[k]
        return carry

    lax.fori_loop(0, groups, group, 0)

    @pl.when(step == pl.num_programs(0) - 1)
    def _():
        sub = iota((SUBLANES, LANES), 0)

        def finish(g, carry):
            v = [top_ref[g, k] for k in range(TOPK)]
            for d in (4, 2, 1):
                v = best_of(v, [pltpu.roll(x, d, 0) for x in v])
            tiles = []
            for i in range(0, TOPK, SUBLANES):
                x = v[i]
                for k in range(1, SUBLANES):
                    x = jnp.where(sub == k, v[i + k], x)
                tiles.append(x)
            tiles = jnp.concatenate(tiles * (LANES // TOPK), axis=0)
            turned_ref[pl.ds(pl.multiple_of(g * LANES, LANES), LANES), :] = tiles.T
            return carry

        lax.fori_loop(0, groups, finish, 0)
        lane = iota((sources, LANES), 1) // TOPK
        per = LANES // TOPK
        for i in range(0, slots, per):
            built = turned_ref[pl.ds(i, sources, stride=slots), :]
            for k in range(1, per):
                x = turned_ref[pl.ds(i + k, sources, stride=slots), :]
                built = jnp.where(lane == k, x, built)
            out_ref[:, i * TOPK : (i + per) * TOPK] = built


def home_kernel(wide_ref, narrow_ref, cand_ref, rank_ref, down_ref, up_ref):
    sources = wide_ref.shape[0]
    returned = jnp.concatenate([wide_ref[...], narrow_ref[...]], axis=1)
    parts, rest = [], returned
    for _ in range(3):
        parts.append(rest.astype(bf16))
        rest = rest - parts[-1].astype(f32)
    cand, rank = cand_ref[...], rank_ref[...]
    shard = iota((sources, LANES), 0)
    flip = (iota((TOPK, TOPK), 0) + iota((TOPK, TOPK), 1) == TOPK - 1).astype(f32).astype(bf16)

    def chosen(c, backwards):
        mine = (cand[c : c + 1, :] == shard).astype(f32).astype(bf16)
        split = []
        for part in parts:
            all_ranks = dot(part, mine, ((0,), (0,)))
            best = all_ranks[:TOPK]
            for r in range(1, WIDE + NARROW):
                best = jnp.where(rank[c : c + 1, :] == r, all_ranks[r * TOPK : (r + 1) * TOPK], best)
            split.append(dot(flip, best.astype(bf16)) if backwards else best)
        return split[0] + split[1] + split[2]

    one = bitonic_rows(jnp.maximum(chosen(0, False), chosen(1, True)), True)
    two = bitonic_rows(jnp.maximum(chosen(2, False), chosen(3, True)), False)
    joined = jnp.maximum(one, two)
    down_ref[...] = bitonic_rows(joined, True)
    up_ref[...] = bitonic_rows(joined, False)


def final_kernel(a_ref, b_ref, c_ref, d_ref, out_ref):
    one = bitonic_rows(jnp.maximum(a_ref[...], b_ref[...]), True)
    two = bitonic_rows(jnp.maximum(c_ref[...], d_ref[...]), False)
    best = bitonic_rows(jnp.maximum(one, two), True)
    turned = jnp.concatenate([best] * (LANES // TOPK), axis=0).T
    out_ref[...] = turned[:, :TOPK]


def shift(x, axis, by):
    n = lax.axis_size(axis)
    return lax.ppermute(x, axis, [(i, (i + by) % n) for i in range(n)])


def exchange_train(x):
    return lax.all_to_all(x, "train", split_axis=0, concat_axis=0, tiled=True)


def over_tiles(x):
    n = x.shape[0] // 2
    a, b = x[:n], x[n:]
    left_a, right_b = shift(a, "tile", 1), shift(b, "tile", -1)
    left_b, right_a = shift(b, "tile", 1), shift(a, "tile", -1)
    far_a, far_b = shift(left_a, "tile", 1), shift(right_b, "tile", -1)
    return a, b, left_a, left_b, right_a, right_b, far_a, far_b


def call(kernel, shapes, **kwargs):
    return pl.pallas_call(
        kernel,
        out_shape=shapes,
        compiler_params=pltpu.CompilerParams(vmem_limit_bytes=VMEM_LIMIT),
        **kwargs,
    )


def scores(meta, train_grads, q, slots, sources):
    rows, features = train_grads.shape
    columns = slots * sources
    whole = [pl.BlockSpec(x.shape, lambda i: (0, 0)) for x in q]
    return pl.pallas_call(
        functools.partial(score_kernel, slots),
        out_shape=jax.ShapeDtypeStruct((sources, slots * TOPK), f32),
        grid=(rows // ROW_BLOCK,),
        in_specs=[
            pl.BlockSpec(memory_space=pltpu.SMEM),
            pl.BlockSpec((ROW_BLOCK, features), lambda i: (i, 0)),
            *whole,
        ],
        out_specs=pl.BlockSpec((sources, slots * TOPK), lambda i: (0, 0)),
        scratch_shapes=[
            pltpu.VMEM((ROW_BLOCK, columns), f32),
            pltpu.VMEM((columns // LANES, TOPK, SUBLANES, LANES), f32),
            pltpu.VMEM((columns, LANES), f32),
        ],
        compiler_params=pltpu.CompilerParams(vmem_limit_bytes=VMEM_LIMIT),
    )(meta, train_grads, *q)


def shards(test_grads, fisher, train_grads, candidates, shard_rows):
    sources = lax.axis_size("train")
    q_rows, features = test_grads.shape
    cand = candidates.T
    cand_count = cand.shape[0]
    me = lax.axis_index("tile")
    meta = jnp.stack([me.astype(i32), shard_rows[0] - me * train_grads.shape[0]])
    first, second, rank = call(
        dispatch_kernel,
        (
            jax.ShapeDtypeStruct((sources * WIDE, features), bf16),
            jax.ShapeDtypeStruct((sources * WIDE, features // 2), bf16),
            jax.ShapeDtypeStruct((cand_count, q_rows), i32),
        ),
    )(test_grads, fisher, cand)
    first = exchange_train(first.reshape(sources, WIDE, features))
    second = exchange_train(second.reshape(sources, WIDE, features // 2))
    wide = over_tiles(first.reshape(sources * WIDE, features))
    second = call(unfold_kernel, jax.ShapeDtypeStruct((sources * NARROW, features), bf16))(
        second.reshape(sources * WIDE, features // 2)
    )
    narrow = over_tiles(second)
    wide = scores(meta, train_grads, wide, WIDE, sources)
    narrow = scores(meta, train_grads, narrow, NARROW, sources)
    wide = exchange_train(wide)
    narrow = exchange_train(narrow)
    best = jax.ShapeDtypeStruct((TOPK, q_rows), f32)
    down, up = call(home_kernel, (best, best))(wide, narrow, cand, rank)
    return call(final_kernel, jax.ShapeDtypeStruct((q_rows, TOPK), f32))(
        down, shift(up, "tile", 1), shift(down, "tile", 2), shift(up, "tile", 3)
    )


def solution(mesh):
    placed = (
        P("train", "tile"),
        P("tile", None, None),
        P(("train", "tile"), None),
        P("train", None),
        P("train"),
    )
    return jax.shard_map(
        shards, mesh=mesh, in_specs=placed, out_specs=P("train", None), check_vma=False
    )
```

profile of v0, /device:TPU:1, one launch (start us, length us, event | category | flops | bytes accessed | tf_op | source)
XLA Modules:
  0.0 173.3 jit_solution(11556209676698145593)
XLA Ops:
  0.0 3.3 %shard_map.55 = (bf16[512,1024]{1,0:T(8,128)(2,1)}, bf16[512,512]{1,0:T(8,128)(2,1)}, s32[4,128]{1,0:T(4,128)}) custom-call(bf16[128,1024]{1,0:T(8,128)(2,1)} %grads_ref.1, bf16[2,512,512]{2,1,0:T(8,128)(2,1)} %fisher_ref.1, s32[4,128]{1,0:T(4,128)} %bitcast.27), custom_call_target="tpu_custom_call" | custom-call | tf_op jit(solution)/shard_map/pallas_call | solution.py:294
  3.3 41.7 %all_to_all.32 = bf16[64,8,1024]{2,1,0:T(8,128)(2,1)S(1)} all-to-all(bf16[64,8,1024]{2,1,0:T(8,128)(2,1)} %bitcast.21), channel_id=1, replica_groups=mesh['train'=64,'tile'=4] {'train'}, dimensions={0} | all-to-all | bytes 2097152 | tf_op jit(solution)/shard_map/all_to_all | solution.py:243
  45.0 6.2 %all-to-all-start.2 = ((bf16[64,8,512]{2,1,0:T(8,128)(2,1)}), bf16[64,8,512]{2,1,0:T(8,128)(2,1)S(1)}, u32[]{:S(2)}, u32[]{:S(2)}) async-start(bf16[64,8,512]{2,1,0:T(8,128)(2,1)} %bitcast.22), calls=%async_computation.2 | async-start | bytes 1048576 | tf_op jit(solution)/shard_map/all_to_all | solution.py:243
  51.2 0.1 slice_bitcast_fusion
  51.3 0.0 copy-start
  51.3 0.0 copy-start.1
  51.3 2.6 %collective-permute-start.3 = (bf16[256,1024]{1,0:T(8,128)(2,1)S(1)}, bf16[256,1024]{1,0:T(8,128)(2,1)S(1)}, u32[]{:S(2)}, u32[]{:S(2)}) collective-permute-start(bf16[256,1024]{1,0:T(8,128)(2,1)S(1)} %get-tuple-element.15.refs_1_), channel_id=1, source_target_pairs={{0,3},{1,0},{2,1},{3,2},{4,7},{5,4},{6,5},{7,6},{8,11},{9,8},{10,9... | collective-permute-start | bytes 1572872 | tf_op jit(solution)/shard_map/ppermute | solution.py:239
  53.9 0.0 collective-permute-start
  53.9 14.7 %all-to-all-done.2 = bf16[64,8,512]{2,1,0:T(8,128)(2,1)S(1)} async-done(((bf16[64,8,512]{2,1,0:T(8,128)(2,1)}), bf16[64,8,512]{2,1,0:T(8,128)(2,1)S(1)}, u32[]{:S(2)}, u32[]{:S(2)}) %all-to-all-start.2) | async-done | bytes 524320 | tf_op jit(solution)/shard_map/all_to_all | solution.py:243
  68.6 0.8 copy-done.2
  69.4 2.0 %shard_map.57 = bf16[256,1024]{1,0:T(8,128)(2,1)} custom-call(bf16[512,512]{1,0:T(8,128)(2,1)} %bitcast.20), custom_call_target="tpu_custom_call" | custom-call | tf_op jit(solution)/shard_map/pallas_call | solution.py:305
  71.3 1.1 fusion
  72.4 0.0 copy-start.3
  72.4 0.0 copy-start.4
  72.4 2.6 %collective-permute-start.9 = (bf16[128,1024]{1,0:T(8,128)(2,1)S(1)}, bf16[128,1024]{1,0:T(8,128)(2,1)S(1)}, u32[]{:S(2)}, u32[]{:S(2)}) collective-permute-start(bf16[128,1024]{1,0:T(8,128)(2,1)S(1)} %get-tuple-element.17.refs_1_), channel_id=1, source_target_pairs={{0,3},{1,0},{2,1},{3,2},{4,7},{5,4},{6,5},{7,6},{8,11},{9,8},{10,9... | collective-permute-start | bytes 786440 | tf_op jit(solution)/shard_map/ppermute | solution.py:239
  75.0 0.0 collective-permute-start.1
  75.0 2.7 %collective-permute-start.2 = (bf16[256,1024]{1,0:T(8,128)(2,1)S(1)}, bf16[256,1024]{1,0:T(8,128)(2,1)S(1)}, u32[]{:S(2)}, u32[]{:S(2)}) collective-permute-start(bf16[256,1024]{1,0:T(8,128)(2,1)S(1)} %get-tuple-element.16.refs_0_), channel_id=1, source_target_pairs={{0,3},{1,0},{2,1},{3,2},{4,7},{5,4},{6,5},{7,6},{8,11},{9,8},{10,9... | collective-permute-start | bytes 1572872 | tf_op jit(solution)/shard_map/ppermute | solution.py:239
  77.6 0.0 collective-permute-done.3.refs_5_
  77.6 0.1 collective-permute-start.5
  77.7 0.0 collective-permute-done.refs_2_
  77.7 1.4 collective-permute-start.4
  79.1 1.2 collective-permute-done.9.refs_5_
  80.3 0.9 collective-permute-start.6
  81.3 24.7 %collective-permute-done.6.refs_2_ = bf16[128,1024]{1,0:T(8,128)(2,1)} collective-permute-done((bf16[128,1024]{1,0:T(8,128)(2,1)S(1)}, bf16[128,1024]{1,0:T(8,128)(2,1)}, u32[]{:S(2)}, u32[]{:S(2)}) %collective-permute-start.6) | collective-permute-done | bytes 262176 | tf_op jit(solution)/shard_map/ppermute | solution.py:239
  106.0 0.0 collective-permute-start.7
  106.0 0.0 collective-permute-done.1.refs_3_
  106.0 2.7 %collective-permute-start.8 = (bf16[128,1024]{1,0:T(8,128)(2,1)S(1)}, bf16[128,1024]{1,0:T(8,128)(2,1)}, u32[]{:S(2)}, u32[]{:S(2)}) collective-permute-start(bf16[128,1024]{1,0:T(8,128)(2,1)S(1)} %get-tuple-element.18.refs_0_), channel_id=1, source_target_pairs={{0,3},{1,0},{2,1},{3,2},{4,7},{5,4},{6,5},{7,6},{8,11},{9,8},{10,9... | collective-permute-start | bytes 786440 | tf_op jit(solution)/shard_map/ppermute | solution.py:239
  108.7 0.0 collective-permute-done.2.refs_4_
  108.7 0.1 collective-permute-start.11
  108.8 0.0 collective-permute-done.5.refs_7_
  108.8 0.7 copy-done.8
  109.5 0.9 collective-permute-start.10
  110.4 0.0 copy-done.9
  111.1 0.6 pad_add_fusion.meta_ref
  111.7 0.0 collective-permute-done.4.refs_6_
  111.7 0.0 copy-done
  111.7 0.0 copy-done.1
  111.7 0.0 copy-done.5
  111.7 0.0 copy-done.6
  111.7 0.0 copy-done.7
  111.7 11.0 %shard_map.56 = f32[64,256]{1,0:T(8,128)} custom-call(s32[2]{0:T(128)} %pad_add_fusion.meta_ref, bf16[1024,4096]{1,0:T(8,128)(2,1)} %train_ref.3, bf16[256,1024]{1,0:T(8,128)(2,1)} %copy-done.1, bf16[256,1024]{1,0:T(8,128)(2,1)} %copy-done, bf16[256,1024]{1,0:T(8,128)(2,1)} %copy-done.6, bf16[256,1024]{1,0:T(8,128)(2,1)} %copy-done.7, ...), custom_call_target="tpu_custom_call" | custom-call | tf_op jit(solution)/shard_map/pallas_call | solution.py:268
  122.7 1.5 copy.7
  124.3 8.2 %all-to-all-start.1 = ((f32[64,1,256]{2,1,0:T(1,128)}), f32[64,1,256]{2,1,0:T(1,128)S(1)}, u32[]{:S(2)}, u32[]{:S(2)}) async-start(f32[64,1,256]{2,1,0:T(1,128)} %copy.7), calls=%async_computation.1 | async-start | bytes 131072 | tf_op jit(solution)/shard_map/all_to_all | solution.py:243
  132.5 0.0 collective-permute-done.7.refs_3_
  132.5 0.0 collective-permute-done.8.refs_4_
  132.5 0.0 collective-permute-done.11.refs_7_
  132.5 0.0 collective-permute-done.10.refs_6_
  132.6 7.8 %shard_map.58 = f32[64,128]{1,0:T(8,128)} custom-call(s32[2]{0:T(128)} %pad_add_fusion.meta_ref, bf16[1024,4096]{1,0:T(8,128)(2,1)} %train_ref.3, bf16[128,1024]{1,0:T(8,128)(2,1)} %copy-done.4, bf16[128,1024]{1,0:T(8,128)(2,1)} %copy-done.3, bf16[128,1024]{1,0:T(8,128)(2,1)} %collective-permute-done.6.refs_2_, ...), custom_call_target="tpu_custom_call" | custom-call | tf_op jit(solution)/shard_map/pallas_call | solution.py:268
  140.3 1.9 %all-to-all-done.1 = f32[64,1,256]{2,1,0:T(1,128)S(1)} async-done(((f32[64,1,256]{2,1,0:T(1,128)}), f32[64,1,256]{2,1,0:T(1,128)S(1)}, u32[]{:S(2)}, u32[]{:S(2)}) %all-to-all-start.1) | async-done | bytes 65568 | tf_op jit(solution)/shard_map/all_to_all | solution.py:243
  142.3 8.4 %all-to-all-start.3 = ((f32[64,1,128]{2,1,0:T(1,128)}), f32[64,1,128]{2,1,0:T(1,128)S(1)}, u32[]{:S(2)}, u32[]{:S(2)}) async-start(f32[64,1,128]{2,1,0:T(1,128)} %bitcast.25), calls=%async_computation.3 | async-start | bytes 65536 | tf_op jit(solution)/shard_map/all_to_all | solution.py:243
  150.7 0.6 copy.12
  151.3 8.7 %all-to-all-done.3 = f32[64,1,128]{2,1,0:T(1,128)S(1)} async-done(((f32[64,1,128]{2,1,0:T(1,128)}), f32[64,1,128]{2,1,0:T(1,128)S(1)}, u32[]{:S(2)}, u32[]{:S(2)}) %all-to-all-start.3) | async-done | bytes 32800 | tf_op jit(solution)/shard_map/all_to_all | solution.py:243
  160.0 0.6 copy-done.11
  160.6 2.4 %shard_map.59 = (f32[32,128]{1,0:T(8,128)}, f32[32,128]{1,0:T(8,128)}) custom-call(f32[64,256]{1,0:T(8,128)} %bitcast.24, f32[64,128]{1,0:T(8,128)} %bitcast.26, s32[4,128]{1,0:T(4,128)} %bitcast.28, s32[4,128]{1,0:T(4,128)} %get-tuple-element.12.rank_ref), custom_call_target="tpu_custom_call" | custom-call | tf_op jit(solution)/shard_map/pallas_call | solution.py:314
  163.0 0.0 collective-permute-start.13
  163.0 2.7 %collective-permute-start.14 = (f32[32,128]{1,0:T(8,128)}, f32[32,128]{1,0:T(8,128)S(1)}, u32[]{:S(2)}, u32[]{:S(2)}) collective-permute-start(f32[32,128]{1,0:T(8,128)} %get-tuple-element.14), channel_id=1, source_target_pairs={{0,3},{1,0},{2,1},{3,2},{4,7},{5,4},{6,5},{7,6},{8,11},{9,8},{10,9... | collective-permute-start | bytes 49160 | tf_op jit(solution)/shard_map/ppermute | solution.py:239
  165.7 0.0 collective-permute-start.12
  165.7 1.6 collective-permute-done.13.c_ref
  167.3 0.0 collective-permute-done.14.d_ref
  167.3 2.4 %collective-permute-done.12.b_ref = f32[32,128]{1,0:T(8,128)S(1)} collective-permute-done((f32[32,128]{1,0:T(8,128)}, f32[32,128]{1,0:T(8,128)S(1)}, u32[]{:S(2)}, u32[]{:S(2)}) %collective-permute-start.12) | collective-permute-done | bytes 16416 | tf_op jit(solution)/shard_map/ppermute | solution.py:239
  169.7 0.0 copy-done.13
  169.7 0.6 copy-done.14
  170.3 1.5 shard_map.60
  171.8 1.5 copy.9
  (15 shorter events, 0.0 us)
Async XLA Ops:
  45.0 23.5 %all-to-all-start.2 = ((bf16[64,8,512]{2,1,0:T(8,128)(2,1)}), bf16[64,8,512]{2,1,0:T(8,128)(2,1)S(1)}, u32[]{:S(2)}, u32[]{:S(2)}) async-start(bf16[64,8,512]{2,1,0:T(8,128)(2,1)} %bitcast.22), calls=%async_computation.2 | async-start | bytes 1048576 | tf_op jit(solution)/shard_map/all_to_all | solution.py:243
  51.3 60.4 %copy-start = (bf16[256,1024]{1,0:T(8,128)(2,1)}, bf16[256,1024]{1,0:T(8,128)(2,1)S(1)}, u32[]{:S(2)}) copy-start(bf16[256,1024]{1,0:T(8,128)(2,1)S(1)} %get-tuple-element.15.refs_1_) | copy-start | bytes 1572868
  51.3 60.4 %copy-start.1 = (bf16[256,1024]{1,0:T(8,128)(2,1)}, bf16[256,1024]{1,0:T(8,128)(2,1)S(1)}, u32[]{:S(2)}) copy-start(bf16[256,1024]{1,0:T(8,128)(2,1)S(1)} %get-tuple-element.16.refs_0_) | copy-start | bytes 1572868
  51.3 26.3 %collective-permute-start.3 = (bf16[256,1024]{1,0:T(8,128)(2,1)S(1)}, bf16[256,1024]{1,0:T(8,128)(2,1)S(1)}, u32[]{:S(2)}, u32[]{:S(2)}) collective-permute-start(bf16[256,1024]{1,0:T(8,128)(2,1)S(1)} %get-tuple-element.15.refs_1_), channel_id=1, source_target_pairs={{0,3},{1,0},{2,1},{3,2},{4,7},{5,4},{6,5},{7,6},{8,11},{9,8},{10,9... | collective-permute-start | bytes 1572872 | tf_op jit(solution)/shard_map/ppermute | solution.py:239
  53.9 23.8 %collective-permute-start = (bf16[256,1024]{1,0:T(8,128)(2,1)S(1)}, bf16[256,1024]{1,0:T(8,128)(2,1)S(1)}, u32[]{:S(2)}, u32[]{:S(2)}) collective-permute-start(bf16[256,1024]{1,0:T(8,128)(2,1)S(1)} %get-tuple-element.16.refs_0_), channel_id=1, source_target_pairs={{0,1},{1,2},{2,3},{3,0},{4,5},{5,6},{6,7},{7,4},{8,9},{9,10},{10,1... | collective-permute-start | bytes 1572872 | tf_op jit(solution)/shard_map/ppermute | solution.py:239
  68.6 0.8 copy-start.2
  72.4 60.2 %copy-start.3 = (bf16[128,1024]{1,0:T(8,128)(2,1)}, bf16[128,1024]{1,0:T(8,128)(2,1)S(1)}, u32[]{:S(2)}) copy-start(bf16[128,1024]{1,0:T(8,128)(2,1)S(1)} %get-tuple-element.17.refs_1_) | copy-start | bytes 786436
  72.4 60.2 %copy-start.4 = (bf16[128,1024]{1,0:T(8,128)(2,1)}, bf16[128,1024]{1,0:T(8,128)(2,1)S(1)}, u32[]{:S(2)}) copy-start(bf16[128,1024]{1,0:T(8,128)(2,1)S(1)} %get-tuple-element.18.refs_0_) | copy-start | bytes 786436
  72.4 7.9 %collective-permute-start.9 = (bf16[128,1024]{1,0:T(8,128)(2,1)S(1)}, bf16[128,1024]{1,0:T(8,128)(2,1)S(1)}, u32[]{:S(2)}, u32[]{:S(2)}) collective-permute-start(bf16[128,1024]{1,0:T(8,128)(2,1)S(1)} %get-tuple-element.17.refs_1_), channel_id=1, source_target_pairs={{0,3},{1,0},{2,1},{3,2},{4,7},{5,4},{6,5},{7,6},{8,11},{9,8},{10,9... | collective-permute-start | bytes 786440 | tf_op jit(solution)/shard_map/ppermute | solution.py:239
  75.0 31.0 %collective-permute-start.1 = (bf16[256,1024]{1,0:T(8,128)(2,1)S(1)}, bf16[256,1024]{1,0:T(8,128)(2,1)S(1)}, u32[]{:S(2)}, u32[]{:S(2)}) collective-permute-start(bf16[256,1024]{1,0:T(8,128)(2,1)S(1)} %get-tuple-element.15.refs_1_), channel_id=1, source_target_pairs={{0,1},{1,2},{2,3},{3,0},{4,5},{5,6},{6,7},{7,4},{8,9},{9,10},{10,1... | collective-permute-start | bytes 1572872 | tf_op jit(solution)/shard_map/ppermute | solution.py:239
  75.0 33.7 %collective-permute-start.2 = (bf16[256,1024]{1,0:T(8,128)(2,1)S(1)}, bf16[256,1024]{1,0:T(8,128)(2,1)S(1)}, u32[]{:S(2)}, u32[]{:S(2)}) collective-permute-start(bf16[256,1024]{1,0:T(8,128)(2,1)S(1)} %get-tuple-element.16.refs_0_), channel_id=1, source_target_pairs={{0,3},{1,0},{2,1},{3,2},{4,7},{5,4},{6,5},{7,6},{8,11},{9,8},{10,9... | collective-permute-start | bytes 1572872 | tf_op jit(solution)/shard_map/ppermute | solution.py:239
  77.6 34.1 %copy-start.5 = (bf16[256,1024]{1,0:T(8,128)(2,1)}, bf16[256,1024]{1,0:T(8,128)(2,1)S(1)}, u32[]{:S(2)}) copy-start(bf16[256,1024]{1,0:T(8,128)(2,1)S(1)} %collective-permute-done.3.refs_5_) | copy-start | bytes 1572868
  77.6 31.1 %collective-permute-start.5 = (bf16[256,1024]{1,0:T(8,128)(2,1)S(1)}, bf16[256,1024]{1,0:T(8,128)(2,1)S(1)}, u32[]{:S(2)}, u32[]{:S(2)}) collective-permute-start(bf16[256,1024]{1,0:T(8,128)(2,1)S(1)} %collective-permute-done.3.refs_5_), channel_id=1, source_target_pairs={{0,3},{1,0},{2,1},{3,2},{4,7},{5,4},{6,5},{7,6},{8,11},{9,8},{10,9... | collective-permute-start | bytes 1572872 | tf_op jit(solution)/shard_map/ppermute | solution.py:239
  77.7 34.0 %copy-start.6 = (bf16[256,1024]{1,0:T(8,128)(2,1)}, bf16[256,1024]{1,0:T(8,128)(2,1)S(1)}, u32[]{:S(2)}) copy-start(bf16[256,1024]{1,0:T(8,128)(2,1)S(1)} %collective-permute-done.refs_2_) | copy-start | bytes 1572868
  77.7 34.0 %collective-permute-start.4 = (bf16[256,1024]{1,0:T(8,128)(2,1)S(1)}, bf16[256,1024]{1,0:T(8,128)(2,1)}, u32[]{:S(2)}, u32[]{:S(2)}) collective-permute-start(bf16[256,1024]{1,0:T(8,128)(2,1)S(1)} %collective-permute-done.refs_2_), channel_id=1, source_target_pairs={{0,1},{1,2},{2,3},{3,0},{4,5},{5,6},{6,7},{7,4},{8,9},{9,10},{10,1... | collective-permute-start | bytes 1572872 | tf_op jit(solution)/shard_map/ppermute | solution.py:239
  80.3 52.2 %copy-start.10 = (bf16[128,1024]{1,0:T(8,128)(2,1)}, bf16[128,1024]{1,0:T(8,128)(2,1)S(1)}, u32[]{:S(2)}) copy-start(bf16[128,1024]{1,0:T(8,128)(2,1)S(1)} %collective-permute-done.9.refs_5_) | copy-start | bytes 786436
  80.3 25.7 %collective-permute-start.6 = (bf16[128,1024]{1,0:T(8,128)(2,1)S(1)}, bf16[128,1024]{1,0:T(8,128)(2,1)}, u32[]{:S(2)}, u32[]{:S(2)}) collective-permute-start(bf16[128,1024]{1,0:T(8,128)(2,1)S(1)} %get-tuple-element.18.refs_0_), channel_id=1, source_target_pairs={{0,1},{1,2},{2,3},{3,0},{4,5},{5,6},{6,7},{7,4},{8,9},{9,10},{10,1... | collective-permute-start | bytes 786440 | tf_op jit(solution)/shard_map/ppermute | solution.py:239
  106.0 26.5 %collective-permute-start.7 = (bf16[128,1024]{1,0:T(8,128)(2,1)S(1)}, bf16[128,1024]{1,0:T(8,128)(2,1)}, u32[]{:S(2)}, u32[]{:S(2)}) collective-permute-start(bf16[128,1024]{1,0:T(8,128)(2,1)S(1)} %get-tuple-element.17.refs_1_), channel_id=1, source_target_pairs={{0,1},{1,2},{2,3},{3,0},{4,5},{5,6},{6,7},{7,4},{8,9},{9,10},{10,1... | collective-permute-start | bytes 786440 | tf_op jit(solution)/shard_map/ppermute | solution.py:239
  106.0 5.7 %copy-start.7 = (bf16[256,1024]{1,0:T(8,128)(2,1)}, bf16[256,1024]{1,0:T(8,128)(2,1)S(1)}, u32[]{:S(2)}) copy-start(bf16[256,1024]{1,0:T(8,128)(2,1)S(1)} %collective-permute-done.1.refs_3_) | copy-start | bytes 1572868
  106.0 26.5 %collective-permute-start.8 = (bf16[128,1024]{1,0:T(8,128)(2,1)S(1)}, bf16[128,1024]{1,0:T(8,128)(2,1)}, u32[]{:S(2)}, u32[]{:S(2)}) collective-permute-start(bf16[128,1024]{1,0:T(8,128)(2,1)S(1)} %get-tuple-element.18.refs_0_), channel_id=1, source_target_pairs={{0,3},{1,0},{2,1},{3,2},{4,7},{5,4},{6,5},{7,6},{8,11},{9,8},{10,9... | collective-permute-start | bytes 786440 | tf_op jit(solution)/shard_map/ppermute | solution.py:239
  108.7 0.8 copy-start.8
  108.7 23.8 %collective-permute-start.11 = (bf16[128,1024]{1,0:T(8,128)(2,1)S(1)}, bf16[128,1024]{1,0:T(8,128)(2,1)}, u32[]{:S(2)}, u32[]{:S(2)}) collective-permute-start(bf16[128,1024]{1,0:T(8,128)(2,1)S(1)} %collective-permute-done.9.refs_5_), channel_id=1, source_target_pairs={{0,3},{1,0},{2,1},{3,2},{4,7},{5,4},{6,5},{7,6},{8,11},{9,8},{10,9... | collective-permute-start | bytes 786440 | tf_op jit(solution)/shard_map/ppermute | solution.py:239
  109.5 0.9 copy-start.9
  109.5 23.1 %collective-permute-start.10 = (bf16[128,1024]{1,0:T(8,128)(2,1)}, bf16[128,1024]{1,0:T(8,128)(2,1)}, u32[]{:S(2)}, u32[]{:S(2)}) collective-permute-start(bf16[128,1024]{1,0:T(8,128)(2,1)} %collective-permute-done.6.refs_2_), channel_id=1, source_target_pairs={{0,1},{1,2},{2,3},{3,0},{4,5},{5,6},{6,7},{7,4},{8,9},{9,10},{10,1... | collective-permute-start | bytes 786440 | tf_op jit(solution)/shard_map/ppermute | solution.py:239
  124.3 18.0 %all-to-all-start.1 = ((f32[64,1,256]{2,1,0:T(1,128)}), f32[64,1,256]{2,1,0:T(1,128)S(1)}, u32[]{:S(2)}, u32[]{:S(2)}) async-start(f32[64,1,256]{2,1,0:T(1,128)} %copy.7), calls=%async_computation.1 | async-start | bytes 131072 | tf_op jit(solution)/shard_map/all_to_all | solution.py:243
  142.3 17.7 %all-to-all-start.3 = ((f32[64,1,128]{2,1,0:T(1,128)}), f32[64,1,128]{2,1,0:T(1,128)S(1)}, u32[]{:S(2)}, u32[]{:S(2)}) async-start(f32[64,1,128]{2,1,0:T(1,128)} %bitcast.25), calls=%async_computation.3 | async-start | bytes 65536 | tf_op jit(solution)/shard_map/all_to_all | solution.py:243
  160.0 0.6 copy-start.11
  163.0 4.3 %collective-permute-start.13 = (f32[32,128]{1,0:T(8,128)}, f32[32,128]{1,0:T(8,128)S(1)}, u32[]{:S(2)}, u32[]{:S(2)}) collective-permute-start(f32[32,128]{1,0:T(8,128)} %get-tuple-element.13.a_ref), channel_id=1, source_target_pairs={{0,2},{1,3},{2,0},{3,1},{4,6},{5,7},{6,4},{7,5},{8,10},{9,11},{10,... | collective-permute-start | bytes 49160 | tf_op jit(solution)/shard_map/ppermute | solution.py:239
  163.0 4.3 %collective-permute-start.14 = (f32[32,128]{1,0:T(8,128)}, f32[32,128]{1,0:T(8,128)S(1)}, u32[]{:S(2)}, u32[]{:S(2)}) collective-permute-start(f32[32,128]{1,0:T(8,128)} %get-tuple-element.14), channel_id=1, source_target_pairs={{0,3},{1,0},{2,1},{3,2},{4,7},{5,4},{6,5},{7,6},{8,11},{9,8},{10,9... | collective-permute-start | bytes 49160 | tf_op jit(solution)/shard_map/ppermute | solution.py:239
  165.7 4.0 %collective-permute-start.12 = (f32[32,128]{1,0:T(8,128)}, f32[32,128]{1,0:T(8,128)S(1)}, u32[]{:S(2)}, u32[]{:S(2)}) collective-permute-start(f32[32,128]{1,0:T(8,128)} %get-tuple-element.14), channel_id=1, source_target_pairs={{0,1},{1,2},{2,3},{3,0},{4,5},{5,6},{6,7},{7,4},{8,9},{9,10},{10,1... | collective-permute-start | bytes 49160 | tf_op jit(solution)/shard_map/ppermute | solution.py:239
  167.3 2.4 %copy-start.12 = (f32[32,128]{1,0:T(8,128)}, f32[32,128]{1,0:T(8,128)S(1)}, u32[]{:S(2)}) copy-start(f32[32,128]{1,0:T(8,128)S(1)} %collective-permute-done.13.c_ref) | copy-start | bytes 49156
  167.3 2.4 %copy-start.13 = (f32[32,128]{1,0:T(8,128)}, f32[32,128]{1,0:T(8,128)S(1)}, u32[]{:S(2)}) copy-start(f32[32,128]{1,0:T(8,128)S(1)} %collective-permute-done.14.d_ref) | copy-start | bytes 49156
  169.7 0.6 copy-start.14
where the time goes:
time: 174 us; the launch traced here: 173 us
  waiting for transfers between devices  55.2 us (32%)
  blocking collectives  41.7 us (24%)
  starting transfers between devices  39.4 us (23%)
  Pallas kernels  28.1 us (16%)
  local copies, waits for them, and re-layouts  7.52 us (4%)
    all_to_all x1, blocking collectives, exchange_train(): return lax.all_to_all(x, 'train', split_axis=0, concat_axis=0, tiled=True)  41.7 us
    ppermute x15, waiting for transfers between devices, shift(): return lax.ppermute(x, axis, [(i, (i + by) % n) for i in range(n)])  30 us
    all_to_all x3, waiting for transfers between devices, exchange_train(): return lax.all_to_all(x, 'train', split_axis=0, concat_axis=0, tiled=True)  25.3 us
    all_to_all x3, starting transfers between devices, exchange_train(): return lax.all_to_all(x, 'train', split_axis=0, concat_axis=0, tiled=True)  22.8 us
    pallas_call x2, Pallas kernels, scores(): pl.pallas_call(functools.partial(score_kernel, slots), out_shape=jax.Shap...  18.8 us
    ppermute x15, starting transfers between devices, shift(): return lax.ppermute(x, axis, [(i, (i + by) % n) for i in range(n)])  16.6 us
  transfers between devices with their start and end apart: 18, of which 7 were waited for; matrix products, arithmetic and copies ran while one was open for 2% of the time, Pallas kernels for 12%

commit v1 on v0

v1 whole, which is shorter than its diff:
```python
import functools

import jax
import jax.numpy as jnp
from jax import lax
from jax.experimental import pallas as pl
from jax.experimental.pallas import tpu as pltpu
from jax.sharding import PartitionSpec as P

TOPK = 32
LOWEST = -1.0e30
LANES = 128
SUBLANES = 8
ROW_BLOCK = TOPK * SUBLANES
WIDE, NARROW = 8, 4
VMEM_LIMIT = 12 * 1024 * 1024

f32, bf16, i32 = jnp.float32, jnp.bfloat16, jnp.int32


def iota(shape, dim):
    return lax.broadcasted_iota(i32, shape, dim)


def dot(a, b, dims=((1,), (0,))):
    return lax.dot_general(a, b, (dims, ((), ())), preferred_element_type=f32)


def sorting_pairs(n):
    pairs, p = [], 1
    while p < n:
        k = p
        while k >= 1:
            for j in range(k % p, n - k, 2 * k):
                for i in range(min(k, n - j - k)):
                    if (i + j) // (2 * p) == (i + j + k) // (2 * p):
                        pairs.append((i + j, i + j + k))
            k //= 2
        p *= 2
    return pairs


def exchange(v, i, j):
    v[i], v[j] = jnp.maximum(v[i], v[j]), jnp.minimum(v[i], v[j])


def sorted_down(v):
    v = list(v)
    for i, j in sorting_pairs(len(v)):
        exchange(v, i, j)
    return v


def bitonic_down(v):
    v, d = list(v), len(v) // 2
    while d:
        for i in range(len(v)):
            if not i & d:
                exchange(v, i, i + d)
        d //= 2
    return v


def best_of(a, b):
    return bitonic_down([jnp.maximum(x, y) for x, y in zip(a, reversed(b))])


def bitonic_rows(x, down):
    v = [x[i : i + SUBLANES] for i in range(0, TOPK, SUBLANES)]
    row = iota((SUBLANES, LANES), 0)
    for d in (2, 1):
        for i in range(len(v)):
            if not i & d:
                high, low = jnp.maximum(v[i], v[i + d]), jnp.minimum(v[i], v[i + d])
                v[i], v[i + d] = (high, low) if down else (low, high)
    for d in (4, 2, 1):
        first = (row & d) == 0
        for i, y in enumerate(v):
            after, before = pltpu.roll(y, SUBLANES - d, 0), pltpu.roll(y, d, 0)
            if down:
                v[i] = jnp.where(first, jnp.maximum(y, after), jnp.minimum(y, before))
            else:
                v[i] = jnp.where(first, jnp.minimum(y, after), jnp.maximum(y, before))
    return jnp.concatenate(v, axis=0)


def dispatch_kernel(
    grads_hbm, fisher_hbm, cand_hbm, first_ref, second_ref, rank_ref, grads_ref, fisher_ref, cand_ref, arrived
):
    copies = [
        pltpu.make_async_copy(source, target, arrived.at[k])
        for k, (source, target) in enumerate(
            ((fisher_hbm, fisher_ref), (grads_hbm, grads_ref), (cand_hbm, cand_ref))
        )
    ]
    for copy in copies:
        copy.start()
    for copy in copies:
        copy.wait()
    q_rows = grads_ref.shape[0]
    blocks, order, _ = fisher_ref.shape
    shards_n = first_ref.shape[0] // WIDE
    precond = jnp.concatenate(
        [
            dot(grads_ref[:, b * order : (b + 1) * order], fisher_ref[b]).astype(bf16)
            for b in range(blocks)
        ],
        axis=1,
    )
    half = blocks * order // 2
    cand = cand_ref[...]
    shard = iota((shards_n, q_rows), 0)
    naming = [cand[c : c + 1, :] == shard for c in range(cand.shape[0])]
    named = functools.reduce(jnp.logical_or, naming)
    before = (iota((q_rows, q_rows), 0) < iota((q_rows, q_rows), 1)).astype(f32).astype(bf16)
    rank = dot(named.astype(f32).astype(bf16), before)
    for c, here in enumerate(naming):
        at = jnp.sum(jnp.where(here, rank, 0.0), axis=0, keepdims=True)
        rank_ref[c : c + 1, :] = at.astype(i32)
    table = jnp.where(named, rank, 255.0).astype(bf16)
    rows = shards_n * WIDE
    spread = (iota((rows, shards_n), 0) // WIDE == iota((rows, shards_n), 1)).astype(f32)
    place = dot(spread.astype(bf16), table)
    row = iota((rows, q_rows), 0)
    pick = (place == (row % WIDE).astype(f32)).astype(f32).astype(bf16)
    first_ref[...] = dot(pick, precond).astype(bf16)
    pick = (place == (row % NARROW + WIDE).astype(f32)).astype(f32).astype(bf16)
    both = dot(pick, precond)
    upper = iota((rows, half), 0) // NARROW % 2 == 0
    second_ref[...] = jnp.where(upper, both[:, :half], both[:, half:]).astype(bf16)


def unfold_kernel(folded_ref, left_ref, right_ref, rows_ref, up_ref, down_ref):
    half = folded_ref.shape[1]
    ahead = left_ref.shape[0] // 2
    upper = iota((SUBLANES, half), 0) < NARROW
    for i in range(0, rows_ref.shape[0], 2 * SUBLANES):
        x = folded_ref[2 * i : 2 * i + 4 * SUBLANES, :].astype(f32)
        built = []
        for k in (0, 2):
            a = x[k * SUBLANES : (k + 1) * SUBLANES]
            b = x[(k + 1) * SUBLANES : (k + 2) * SUBLANES]
            left = jnp.where(upper, a, pltpu.roll(b, NARROW, 0))
            right = jnp.where(upper, pltpu.roll(a, NARROW, 0), b)
            built.append(jnp.concatenate([left, right], axis=1))
        built = jnp.concatenate(built, axis=0).astype(bf16)
        rows_ref[i : i + 2 * SUBLANES, :] = built
        up_ref[ahead + i : ahead + i + 2 * SUBLANES, :] = built
        down_ref[ahead + i : ahead + i + 2 * SUBLANES, :] = built
    up_ref[:ahead, :] = left_ref[:ahead, :]
    down_ref[:ahead, :] = right_ref[ahead:, :]


AWAY = (0, 3, 1, 2)


def partial_kernel(meta_ref, rows_ref, own_ref, left_ref, right_ref, train_ref, sum_ref, arrived):
    me = meta_ref[0]
    width = train_ref.shape[2]
    copies = []
    for j, away in enumerate(AWAY):
        columns = pl.ds(pl.multiple_of(((me + away) & 3) * width, width), width)
        copies.append(
            pltpu.make_async_copy(rows_ref.at[:, columns], train_ref.at[j], arrived.at[j])
        )
        copies[-1].start()
    total = None
    for j, ref in enumerate((own_ref, left_ref, right_ref)):
        copies[j].wait()
        part = dot(train_ref[j], ref[...], ((1,), (1,)))
        total = part if total is None else total + part
    sum_ref[...] = total
    copies[3].wait()


def select(slots, live, sum_ref, turned_ref, write):
    rows, columns = sum_ref.shape
    sources = columns // slots
    sub = iota((SUBLANES, LANES), 0)

    def group(g, carry):
        lanes = pl.ds(pl.multiple_of(g * LANES, LANES), LANES)
        best = None
        for i in range(0, rows, ROW_BLOCK):
            v = []
            for k in range(i, i + ROW_BLOCK, SUBLANES):
                v.append(jnp.where(sub < live - k, sum_ref[k : k + SUBLANES, lanes], LOWEST))
            v = sorted_down(v)
            best = v if best is None else best_of(best, v)
        for d in (4, 2, 1):
            best = best_of(best, [pltpu.roll(x, d, 0) for x in best])
        tiles = []
        for i in range(0, TOPK, SUBLANES):
            x = best[i]
            for k in range(1, SUBLANES):
                x = jnp.where(sub == k, best[i + k], x)
            tiles.append(x)
        tiles = jnp.concatenate(tiles * (LANES // TOPK), axis=0)
        turned_ref[pl.ds(pl.multiple_of(g * LANES, LANES), LANES), :] = tiles.T
        return carry

    lax.fori_loop(0, columns // LANES, group, 0)
    lane = iota((sources, LANES), 1) // TOPK
    per = LANES // TOPK
    for i in range(0, slots, per):
        built = turned_ref[pl.ds(i, sources, stride=slots), :]
        for k in range(1, per):
            x = turned_ref[pl.ds(i + k, sources, stride=slots), :]
            built = jnp.where(lane == k, x, built)
        write(i * TOPK, built)


def wide_kernel(meta_ref, train_ref, part_ref, up_ref, down_ref, out_ref, sum_ref, turned_ref):
    half = sum_ref.shape[1] // 2
    for k, ref in enumerate((up_ref, down_ref)):
        at = slice(k * half, (k + 1) * half)
        sum_ref[:, at] = part_ref[:, at] + dot(train_ref[3], ref[:half, :], ((1,), (1,)))

    def write(at, built):
        out_ref[:, at : at + LANES] = built

    select(WIDE, meta_ref[1], sum_ref, turned_ref, write)


def narrow_kernel(
    meta_ref, train_ref, own_ref, up_ref, down_ref, far_a_ref, far_b_ref, wide_ref, out_ref, sum_ref, turned_ref
):
    skip = up_ref.shape[0] - sum_ref.shape[1]
    far = jnp.concatenate([far_a_ref[...], far_b_ref[...]], axis=0)
    blocks = (own_ref[...], up_ref[skip:, :], down_ref[skip:, :], far)
    sum_ref[...] = functools.reduce(
        jnp.add, [dot(train_ref[j], q, ((1,), (1,))) for j, q in enumerate(blocks)]
    )
    done = wide_ref.shape[1]
    out_ref[:, 0, :done] = wide_ref[...]

    def write(at, built):
        out_ref[:, 0, done + at : done + at + LANES] = built

    select(NARROW, meta_ref[1], sum_ref, turned_ref, write)


def turned_over(x):
    v = [x[i : i + SUBLANES] for i in range(TOPK - SUBLANES, -1, -SUBLANES)]
    row = iota((SUBLANES, LANES), 0)
    for d in (4, 2, 1):
        first = (row & d) == 0
        v = [jnp.where(first, pltpu.roll(y, SUBLANES - d, 0), pltpu.roll(y, d, 0)) for y in v]
    return jnp.concatenate(v, axis=0)


def home_kernel(returned_ref, cand_ref, rank_ref, down_ref, up_ref):
    sources = returned_ref.shape[0]
    rest = returned_ref[:, 0, :]
    cand, rank = cand_ref[...], rank_ref[...]
    shard = iota((sources, LANES), 0)
    mine = jnp.concatenate(
        [(cand[c : c + 1, :] == shard).astype(f32).astype(bf16) for c in range(cand.shape[0])], axis=1
    )
    found = None
    for _ in range(3):
        part = rest.astype(bf16)
        rest = rest - part.astype(f32)
        x = dot(part, mine, ((0,), (0,)))
        found = x if found is None else found + x

    def chosen(c):
        at = slice(c * LANES, (c + 1) * LANES)
        best = found[:TOPK, at]
        for r in range(1, WIDE + NARROW):
            best = jnp.where(rank[c : c + 1, :] == r, found[r * TOPK : (r + 1) * TOPK, at], best)
        return best

    one = bitonic_rows(jnp.maximum(chosen(0), turned_over(chosen(1))), True)
    two = bitonic_rows(jnp.maximum(chosen(2), turned_over(chosen(3))), False)
    joined = jnp.maximum(one, two)
    down_ref[...] = bitonic_rows(joined, True)
    up_ref[...] = bitonic_rows(joined, False)


def final_kernel(a_ref, b_ref, c_ref, d_ref, out_ref):
    one = bitonic_rows(jnp.maximum(a_ref[...], b_ref[...]), True)
    two = bitonic_rows(jnp.maximum(c_ref[...], d_ref[...]), False)
    out_ref[...] = bitonic_rows(jnp.maximum(one, two), True)


def shift(x, axis, by):
    n = lax.axis_size(axis)
    return lax.ppermute(x, axis, [(i, (i + by) % n) for i in range(n)])


def exchange_train(x):
    return lax.all_to_all(x, "train", split_axis=0, concat_axis=0, tiled=True)


def near(x):
    return shift(x, "tile", 1), shift(x, "tile", -1)


SMEM, HBM, VMEM = (pl.BlockSpec(memory_space=x) for x in (pltpu.SMEM, pltpu.HBM, pltpu.VMEM))


def call(kernel, shapes, *operands, spaces=None, scratch=(), limit=VMEM_LIMIT):
    spaces = [VMEM] * len(operands) if spaces is None else spaces
    return pl.pallas_call(
        kernel,
        out_shape=shapes,
        in_specs=spaces,
        out_specs=jax.tree.map(lambda _: VMEM, shapes),
        scratch_shapes=scratch,
        compiler_params=pltpu.CompilerParams(vmem_limit_bytes=limit),
    )(*operands)


def in_hbm(x):
    return pltpu.with_memory_space_constraint(x, pltpu.HBM)


def shards(test_grads, fisher, train_grads, candidates, shard_rows):
    sources = lax.axis_size("train")
    q_rows, features = test_grads.shape
    rows = train_grads.shape[0]
    cand = candidates.T
    me = lax.axis_index("tile")
    meta = jnp.stack([me.astype(i32), shard_rows[0] - me * rows])
    array = jax.ShapeDtypeStruct
    first, second, rank = call(
        dispatch_kernel,
        (
            array((sources * WIDE, features), bf16),
            array((sources * WIDE, features // 2), bf16),
            array(cand.shape, i32),
        ),
        in_hbm(test_grads),
        in_hbm(fisher),
        in_hbm(cand),
        spaces=[HBM] * 3,
        scratch=[
            pltpu.VMEM(test_grads.shape, bf16),
            pltpu.VMEM(fisher.shape, bf16),
            pltpu.VMEM(cand.shape, i32),
            pltpu.SemaphoreType.DMA((3,)),
        ],
    )
    first = exchange_train(first.reshape(sources, WIDE, features))
    second, first = lax.optimization_barrier((second, first))
    second = exchange_train(second.reshape(sources, WIDE, features // 2))
    first = first.reshape(sources * WIDE, features)
    left, right = near(first)
    second, left, right = lax.optimization_barrier((second, left, right))
    doubled = array((2 * sources * NARROW, features), bf16)
    second, up, down = call(
        unfold_kernel,
        (array((sources * NARROW, features), bf16), doubled, doubled),
        second.reshape(sources * WIDE, features // 2),
        left,
        right,
    )
    after, _ = lax.optimization_barrier((meta, second))
    up, down = shift(up, "tile", 1), shift(down, "tile", -1)
    train, part = call(
        partial_kernel,
        (array((4, rows, features), bf16), array((rows, sources * WIDE), f32)),
        after,
        in_hbm(train_grads),
        first,
        left,
        right,
        spaces=[SMEM, HBM, VMEM, VMEM, VMEM],
        scratch=[pltpu.SemaphoreType.DMA((4,))],
    )
    up, down, part = lax.optimization_barrier((up, down, part))
    start, middle = sources * NARROW, sources * (NARROW + NARROW // 2)
    ends = shift(up[start:middle], "tile", 1), shift(down[middle:], "tile", -1)

    def room(slots):
        columns = slots * sources
        return [pltpu.VMEM((rows, columns), f32), pltpu.VMEM((columns, LANES), f32)]

    wide = call(
        wide_kernel,
        array((sources, WIDE * TOPK), f32),
        meta,
        train,
        part,
        up,
        down,
        spaces=[SMEM] + [VMEM] * 4,
        scratch=room(WIDE),
    )
    both = call(
        narrow_kernel,
        array((sources, 1, (WIDE + NARROW) * TOPK), f32),
        meta,
        train,
        second,
        up,
        down,
        *ends,
        wide,
        spaces=[SMEM] + [VMEM] * 7,
        scratch=room(NARROW),
    )
    both = exchange_train(both)
    best = array((TOPK, q_rows), f32)
    down, up = call(home_kernel, (best, best), both, cand, rank)
    return call(
        final_kernel, best, down, shift(up, "tile", 1), shift(down, "tile", 2), shift(up, "tile", 3)
    ).T


def solution(mesh):
    placed = (
        P("train", "tile"),
        P("tile", None, None),
        P(("train", "tile"), None),
        P("train", None),
        P("train"),
    )
    return jax.shard_map(
        shards, mesh=mesh, in_specs=placed, out_specs=P("train", None), check_vma=False
    )
```

time: 174 us -> 139 us (0.80)
  blocking collectives: 41.7 us -> 85.1 us
  waiting for transfers between devices: 55.2 us -> 20.8 us
  starting transfers between devices: 39.4 us -> 9.28 us
  Pallas kernels: 28.1 us -> 19.8 us
  local copies, waits for them, and re-layouts: 7.52 us -> 3.29 us
    all_to_all x1 -> x3, blocking collectives: 41.7 us -> 85.1 us  [exchange_train(): return lax.all_to_all(x, 'train', split_axis=0, concat_axis=0, tiled=True)]
    all_to_all x3 -> x0, waiting for transfers between devices: 25.3 us -> none  [exchange_train(): return lax.all_to_all(x, 'train', split_axis=0, concat_axis=0, tiled=True)]
    all_to_all x3 -> x0, starting transfers between devices: 22.8 us -> none  [exchange_train(): return lax.all_to_all(x, 'train', split_axis=0, concat_axis=0, tiled=True)]
    ppermute x15 -> x9, waiting for transfers between devices: 30 us -> 20.8 us  [shift(): return lax.ppermute(x, axis, [(i, (i + by) % n) for i in range(n)])]
    pallas_call x6 -> x7, Pallas kernels: 28.1 us -> 19.8 us  [call(): pl.pallas_call(kernel, out_shape=shapes, in_specs=spaces, out_specs=jax.t...]
    ppermute x15 -> x9, starting transfers between devices: 16.6 us -> 9.28 us  [shift(): return lax.ppermute(x, axis, [(i, (i + by) % n) for i in range(n)])]
  transfers between devices with their start and end apart: 18 -> 9, of which waited for: 7 -> 5; matrix products, arithmetic and copies ran while one was open for 2% -> 0% of each run, Pallas kernels for 12% -> 7%
where the time goes in v1:
time: 139 us
  blocking collectives  85.1 us (61%)
  waiting for transfers between devices  20.8 us (15%)
  Pallas kernels  19.8 us (14%)
  starting transfers between devices  9.28 us (7%)
  local copies, waits for them, and re-layouts  3.29 us (2%)
    all_to_all x3, blocking collectives, exchange_train(): return lax.all_to_all(x, 'train', split_axis=0, concat_axis=0, tiled=True)  85.1 us
    ppermute x9, waiting for transfers between devices, shift(): return lax.ppermute(x, axis, [(i, (i + by) % n) for i in range(n)])  20.8 us
    pallas_call x7, Pallas kernels, call(): pl.pallas_call(kernel, out_shape=shapes, in_specs=spaces, out_specs=jax.t...  19.8 us
    ppermute x9, starting transfers between devices, shift(): return lax.ppermute(x, axis, [(i, (i + by) % n) for i in range(n)])  9.28 us
    unnamed x14, local copies, waits for them, and re-layouts  3.26 us
  transfers between devices with their start and end apart: 9, of which 5 were waited for; matrix products, arithmetic and copies ran while one was open for 0% of the time, Pallas kernels for 7%

profile of v1, /device:TPU:1, one launch (start us, length us, event | category | flops | bytes accessed | tf_op | source)
XLA Modules:
  0.0 139.2 jit_solution(15599191555308138305)
XLA Ops:
  0.0 2.4 %shard_map.55 = (bf16[512,1024]{1,0:T(8,128)(2,1)S(1)}, bf16[512,512]{1,0:T(8,128)(2,1)S(1)}, s32[4,128]{1,0:T(4,128)S(1)}) custom-call(bf16[128,1024]{1,0:T(8,128)(2,1)} %grads_hbm.1, bf16[2,512,512]{2,1,0:T(8,128)(2,1)} %fisher_hbm.1, s32[4,128]{1,0:T(4,128)} %bitcast.16), custom_call_target="tpu_custom_call" | custom-call | tf_op jit(solution)/shard_map/pallas_call | solution.py:305
  2.4 41.5 %all_to_all.15 = bf16[64,8,1024]{2,1,0:T(8,128)(2,1)S(1)} all-to-all(bf16[64,8,1024]{2,1,0:T(8,128)(2,1)S(1)} %bitcast.14), channel_id=1, replica_groups=mesh['train'=64,'tile'=4] {'train'}, dimensions={0} | all-to-all | bytes 2097152 | tf_op jit(solution)/shard_map/all_to_all | solution.py:293
  43.9 2.5 %collective-permute-start.1 = (bf16[512,1024]{1,0:T(8,128)(2,1)S(1)}, bf16[512,1024]{1,0:T(8,128)(2,1)S(1)}, u32[]{:S(2)}, u32[]{:S(2)}) collective-permute-start(bf16[512,1024]{1,0:T(8,128)(2,1)S(1)} %bitcast.10), channel_id=1, source_target_pairs={{0,3},{1,0},{2,1},{3,2},{4,7},{5,4},{6,5},{7,6},{8,11},{9,8},{10,9... | collective-permute-start | bytes 3145736 | tf_op jit(solution)/shard_map/ppermute | solution.py:289
  46.4 0.0 collective-permute-start
  46.4 23.6 %all_to_all.16 = bf16[64,8,512]{2,1,0:T(8,128)(2,1)S(1)} all-to-all(bf16[64,8,512]{2,1,0:T(8,128)(2,1)S(1)} %bitcast.15), channel_id=1, replica_groups=mesh['train'=64,'tile'=4] {'train'}, dimensions={0} | all-to-all | bytes 1048576 | tf_op jit(solution)/shard_map/all_to_all | solution.py:293
  70.0 0.0 collective-permute-done.1.right_ref
  70.0 0.0 copy-start
  70.0 2.0 %collective-permute-done.left_ref = bf16[512,1024]{1,0:T(8,128)(2,1)S(1)} collective-permute-done((bf16[512,1024]{1,0:T(8,128)(2,1)S(1)}, bf16[512,1024]{1,0:T(8,128)(2,1)S(1)}, u32[]{:S(2)}, u32[]{:S(2)}) %collective-permute-start) | collective-permute-done | bytes 1048608 | tf_op jit(solution)/shard_map/ppermute | solution.py:289
  72.0 0.0 copy-start.2
  72.0 1.6 %shard_map.56 = (bf16[256,1024]{1,0:T(8,128)(2,1)S(1)}, bf16[512,1024]{1,0:T(8,128)(2,1)}, bf16[512,1024]{1,0:T(8,128)(2,1)}) custom-call(bf16[512,512]{1,0:T(8,128)(2,1)S(1)} %bitcast.13, bf16[512,1024]{1,0:T(8,128)(2,1)S(1)} %collective-permute-done.left_ref, bf16[512,1024]{1,0:T(8,128)(2,1)S(1)} %collective-permute-done.1.right_ref), custom_call_target="tpu_custom_call" | custom-call | tf_op jit(solution)/shard_map/pallas_call | solution.py:305
  73.7 0.0 copy-start.4
  73.7 0.8 copy-done.4
  74.4 0.0 collective-permute-start.2
  74.5 0.0 copy-done
  74.5 0.0 copy-done.2
  74.5 2.7 %collective-permute-start.3 = (bf16[512,1024]{1,0:T(8,128)(2,1)}, bf16[512,1024]{1,0:T(8,128)(2,1)S(1)}, u32[]{:S(2)}, u32[]{:S(2)}) collective-permute-start(bf16[512,1024]{1,0:T(8,128)(2,1)} %get-tuple-element.35), channel_id=1, source_target_pairs={{0,3},{1,0},{2,1},{3,2},{4,7},{5,4},{6,5},{7,6},{8,11},{9,8},{10,9... | collective-permute-start | bytes 3145736 | tf_op jit(solution)/shard_map/ppermute | solution.py:289
  77.8 0.1 pad_add_fusion.meta_ref
  77.9 0.0 copy-start.1
  77.9 1.2 copy-done.1
  79.1 0.0 copy-start.3
  79.1 1.2 copy-done.3
  80.3 6.3 %shard_map.57 = (bf16[4,1024,1024]{2,1,0:T(8,128)(2,1)S(1)}, f32[1024,512]{1,0:T(8,128)S(1)}) custom-call(s32[2]{0:T(128)S(1)} %pad_add_fusion.meta_ref, bf16[1024,4096]{1,0:T(8,128)(2,1)} %rows_ref.1, bf16[512,1024]{1,0:T(8,128)(2,1)S(1)} %bitcast.12, bf16[512,1024]{1,0:T(8,128)(2,1)S(1)} %copy-done.3, bf16[512,1024]{1,0:T(8,128)(2,1)S(1)} %copy-done.1), custom_call_target="tpu_custom_call" | custom-call | tf_op jit(solution)/shard_map/pallas_call | solution.py:305
  86.7 0.0 copy-start.5
  86.7 12.7 %collective-permute-done.2.up_ref = bf16[512,1024]{1,0:T(8,128)(2,1)S(1)} collective-permute-done((bf16[512,1024]{1,0:T(8,128)(2,1)}, bf16[512,1024]{1,0:T(8,128)(2,1)S(1)}, u32[]{:S(2)}, u32[]{:S(2)}) %collective-permute-start.2) | collective-permute-done | bytes 1048608 | tf_op jit(solution)/shard_map/ppermute | solution.py:289
  99.3 0.0 collective-permute-done.3.down_ref
  99.4 2.5 %collective-permute-start.5 = (bf16[128,1024]{1,0:T(8,128)(2,1)S(1)}, bf16[128,1024]{1,0:T(8,128)(2,1)S(1)}, u32[]{:S(2)}, u32[]{:S(2)}) collective-permute-start(bf16[128,1024]{1,0:T(8,128)(2,1)S(1)} %slice.7), channel_id=1, source_target_pairs={{0,3},{1,0},{2,1},{3,2},{4,7},{5,4},{6,5},{7,6},{8,11},{9,8},{10,9... | collective-permute-start | bytes 786440 | tf_op jit(solution)/shard_map/ppermute | solution.py:289
  101.9 0.0 collective-permute-start.4
  101.9 4.0 %shard_map.58.wide_ref = f32[64,256]{1,0:T(8,128)S(1)} custom-call(s32[2]{0:T(128)S(1)} %pad_add_fusion.meta_ref, bf16[4,1024,1024]{2,1,0:T(8,128)(2,1)S(1)} %get-tuple-element.33.train_ref, f32[1024,512]{1,0:T(8,128)S(1)} %get-tuple-element.39.part_ref, bf16[512,1024]{1,0:T(8,128)(2,1)S(1)} %collective-permute-done.2.up_ref, ...), custom_call_target="tpu_custom_call" | custom-call | tf_op jit(solution)/shard_map/pallas_call | solution.py:305
  105.9 0.0 copy-start.6
  105.9 0.0 collective-permute-done.5.far_b_ref
  105.9 2.4 %collective-permute-done.4.far_a_ref = bf16[128,1024]{1,0:T(8,128)(2,1)S(1)} collective-permute-done((bf16[128,1024]{1,0:T(8,128)(2,1)S(1)}, bf16[128,1024]{1,0:T(8,128)(2,1)S(1)}, u32[]{:S(2)}, u32[]{:S(2)}) %collective-permute-start.4) | collective-permute-done | bytes 262176 | tf_op jit(solution)/shard_map/ppermute | solution.py:289
  108.3 0.0 copy-done.5
  108.3 4.0 %shard_map.59 = f32[64,1,384]{2,1,0:T(1,128)S(1)} custom-call(s32[2]{0:T(128)S(1)} %pad_add_fusion.meta_ref, bf16[4,1024,1024]{2,1,0:T(8,128)(2,1)S(1)} %get-tuple-element.33.train_ref, bf16[256,1024]{1,0:T(8,128)(2,1)S(1)} %copy-done.5, bf16[512,1024]{1,0:T(8,128)(2,1)S(1)} %collective-permute-done.2.up_ref, ...), custom_call_target="tpu_custom_call" | custom-call | tf_op jit(solution)/shard_map/pallas_call | solution.py:305
  112.3 20.1 %all_to_all.17.returned_ref = f32[64,1,384]{2,1,0:T(1,128)S(1)} all-to-all(f32[64,1,384]{2,1,0:T(1,128)S(1)} %shard_map.59), channel_id=1, replica_groups=mesh['train'=64,'tile'=4] {'train'}, dimensions={0} | all-to-all | bytes 196608 | tf_op jit(solution)/shard_map/all_to_all | solution.py:293
  132.4 0.0 copy-done.6
  132.4 0.8 shard_map.60
  133.2 0.1 collective-permute-start.7
  133.3 1.2 collective-permute-start.8
  134.5 0.4 collective-permute-start.6
  134.9 2.5 %collective-permute-done.7.c_ref = f32[32,128]{1,0:T(8,128)S(1)} collective-permute-done((f32[32,128]{1,0:T(8,128)S(1)}, f32[32,128]{1,0:T(8,128)S(1)}, u32[]{:S(2)}, u32[]{:S(2)}) %collective-permute-start.7) | collective-permute-done | bytes 16416 | tf_op jit(solution)/shard_map/ppermute | solution.py:289
  137.4 0.0 collective-permute-done.8.d_ref
  137.4 1.1 collective-permute-done.6.b_ref
  138.6 0.6 shard_map.61
  (2 shorter events, 0.0 us)
Async XLA Ops:
  43.9 26.1 %collective-permute-start.1 = (bf16[512,1024]{1,0:T(8,128)(2,1)S(1)}, bf16[512,1024]{1,0:T(8,128)(2,1)S(1)}, u32[]{:S(2)}, u32[]{:S(2)}) collective-permute-start(bf16[512,1024]{1,0:T(8,128)(2,1)S(1)} %bitcast.10), channel_id=1, source_target_pairs={{0,3},{1,0},{2,1},{3,2},{4,7},{5,4},{6,5},{7,6},{8,11},{9,8},{10,9... | collective-permute-start | bytes 3145736 | tf_op jit(solution)/shard_map/ppermute | solution.py:289
  46.4 25.6 %collective-permute-start = (bf16[512,1024]{1,0:T(8,128)(2,1)S(1)}, bf16[512,1024]{1,0:T(8,128)(2,1)S(1)}, u32[]{:S(2)}, u32[]{:S(2)}) collective-permute-start(bf16[512,1024]{1,0:T(8,128)(2,1)S(1)} %bitcast.11), channel_id=1, source_target_pairs={{0,1},{1,2},{2,3},{3,0},{4,5},{5,6},{6,7},{7,4},{8,9},{9,10},{10,1... | collective-permute-start | bytes 3145736 | tf_op jit(solution)/shard_map/ppermute | solution.py:289
  70.0 4.4 %copy-start = (bf16[512,1024]{1,0:T(8,128)(2,1)}, bf16[512,1024]{1,0:T(8,128)(2,1)S(1)}, u32[]{:S(2)}) copy-start(bf16[512,1024]{1,0:T(8,128)(2,1)S(1)} %collective-permute-done.1.right_ref) | copy-start | bytes 3145732
  72.0 2.4 %copy-start.2 = (bf16[512,1024]{1,0:T(8,128)(2,1)}, bf16[512,1024]{1,0:T(8,128)(2,1)S(1)}, u32[]{:S(2)}) copy-start(bf16[512,1024]{1,0:T(8,128)(2,1)S(1)} %collective-permute-done.left_ref) | copy-start | bytes 3145732
  73.7 0.8 copy-start.4
  74.4 24.9 %collective-permute-start.2 = (bf16[512,1024]{1,0:T(8,128)(2,1)}, bf16[512,1024]{1,0:T(8,128)(2,1)S(1)}, u32[]{:S(2)}, u32[]{:S(2)}) collective-permute-start(bf16[512,1024]{1,0:T(8,128)(2,1)} %get-tuple-element.34), channel_id=1, source_target_pairs={{0,1},{1,2},{2,3},{3,0},{4,5},{5,6},{6,7},{7,4},{8,9},{9,10},{10,1... | collective-permute-start | bytes 3145736 | tf_op jit(solution)/shard_map/ppermute | solution.py:289
  74.5 24.9 %collective-permute-start.3 = (bf16[512,1024]{1,0:T(8,128)(2,1)}, bf16[512,1024]{1,0:T(8,128)(2,1)S(1)}, u32[]{:S(2)}, u32[]{:S(2)}) collective-permute-start(bf16[512,1024]{1,0:T(8,128)(2,1)} %get-tuple-element.35), channel_id=1, source_target_pairs={{0,3},{1,0},{2,1},{3,2},{4,7},{5,4},{6,5},{7,6},{8,11},{9,8},{10,9... | collective-permute-start | bytes 3145736 | tf_op jit(solution)/shard_map/ppermute | solution.py:289
  77.9 1.2 copy-start.1
  79.1 1.2 copy-start.3
  86.7 21.7 %copy-start.5 = (bf16[256,1024]{1,0:T(8,128)(2,1)S(1)}, bf16[256,1024]{1,0:T(8,128)(2,1)}, u32[]{:S(2)}) copy-start(bf16[256,1024]{1,0:T(8,128)(2,1)} %copy-done.4) | copy-start | bytes 1572868
  99.4 6.5 %collective-permute-start.5 = (bf16[128,1024]{1,0:T(8,128)(2,1)S(1)}, bf16[128,1024]{1,0:T(8,128)(2,1)S(1)}, u32[]{:S(2)}, u32[]{:S(2)}) collective-permute-start(bf16[128,1024]{1,0:T(8,128)(2,1)S(1)} %slice.7), channel_id=1, source_target_pairs={{0,3},{1,0},{2,1},{3,2},{4,7},{5,4},{6,5},{7,6},{8,11},{9,8},{10,9... | collective-permute-start | bytes 786440 | tf_op jit(solution)/shard_map/ppermute | solution.py:289
  101.9 6.4 %collective-permute-start.4 = (bf16[128,1024]{1,0:T(8,128)(2,1)S(1)}, bf16[128,1024]{1,0:T(8,128)(2,1)S(1)}, u32[]{:S(2)}, u32[]{:S(2)}) collective-permute-start(bf16[128,1024]{1,0:T(8,128)(2,1)S(1)} %slice.6), channel_id=1, source_target_pairs={{0,1},{1,2},{2,3},{3,0},{4,5},{5,6},{6,7},{7,4},{8,9},{9,10},{10,1... | collective-permute-start | bytes 786440 | tf_op jit(solution)/shard_map/ppermute | solution.py:289
  105.9 26.5 %copy-start.6 = (s32[128,4]{0,1:T(4,128)S(1)}, s32[128,4]{0,1:T(4,128)}, u32[]{:S(2)}) copy-start(s32[128,4]{0,1:T(4,128)} %param.8) | copy-start | bytes 6148
  133.2 4.2 %collective-permute-start.7 = (f32[32,128]{1,0:T(8,128)S(1)}, f32[32,128]{1,0:T(8,128)S(1)}, u32[]{:S(2)}, u32[]{:S(2)}) collective-permute-start(f32[32,128]{1,0:T(8,128)S(1)} %get-tuple-element.41.a_ref), channel_id=1, source_target_pairs={{0,2},{1,3},{2,0},{3,1},{4,6},{5,7},{6,4},{7,5},{8,10},{9,11},{10,... | collective-permute-start | bytes 49160 | tf_op jit(solution)/shard_map/ppermute | solution.py:289
  133.3 4.1 %collective-permute-start.8 = (f32[32,128]{1,0:T(8,128)S(1)}, f32[32,128]{1,0:T(8,128)S(1)}, u32[]{:S(2)}, u32[]{:S(2)}) collective-permute-start(f32[32,128]{1,0:T(8,128)S(1)} %get-tuple-element.42), channel_id=1, source_target_pairs={{0,3},{1,0},{2,1},{3,2},{4,7},{5,4},{6,5},{7,6},{8,11},{9,8},{10,9... | collective-permute-start | bytes 49160 | tf_op jit(solution)/shard_map/ppermute | solution.py:289
  134.5 4.1 %collective-permute-start.6 = (f32[32,128]{1,0:T(8,128)S(1)}, f32[32,128]{1,0:T(8,128)S(1)}, u32[]{:S(2)}, u32[]{:S(2)}) collective-permute-start(f32[32,128]{1,0:T(8,128)S(1)} %get-tuple-element.42), channel_id=1, source_target_pairs={{0,1},{1,2},{2,3},{3,0},{4,5},{5,6},{6,7},{7,4},{8,9},{9,10},{10,1... | collective-permute-start | bytes 49160 | tf_op jit(solution)/shard_map/ppermute | solution.py:289

commit v2 on v1

--- a/solution.py
+++ b/solution.py
@@ -130,9 +130,8 @@
     second_ref[...] = jnp.where(upper, both[:, :half], both[:, half:]).astype(bf16)
 
 
-def unfold_kernel(folded_ref, left_ref, right_ref, rows_ref, up_ref, down_ref):
+def unfold_kernel(folded_ref, rows_ref):
     half = folded_ref.shape[1]
-    ahead = left_ref.shape[0] // 2
     upper = iota((SUBLANES, half), 0) < NARROW
     for i in range(0, rows_ref.shape[0], 2 * SUBLANES):
         x = folded_ref[2 * i : 2 * i + 4 * SUBLANES, :].astype(f32)
@@ -143,20 +142,17 @@
             left = jnp.where(upper, a, pltpu.roll(b, NARROW, 0))
             right = jnp.where(upper, pltpu.roll(a, NARROW, 0), b)
             built.append(jnp.concatenate([left, right], axis=1))
-        built = jnp.concatenate(built, axis=0).astype(bf16)
-        rows_ref[i : i + 2 * SUBLANES, :] = built
-        up_ref[ahead + i : ahead + i + 2 * SUBLANES, :] = built
-        down_ref[ahead + i : ahead + i + 2 * SUBLANES, :] = built
-    up_ref[:ahead, :] = left_ref[:ahead, :]
-    down_ref[:ahead, :] = right_ref[ahead:, :]
+        rows_ref[i : i + 2 * SUBLANES, :] = jnp.concatenate(built, axis=0).astype(bf16)
 
 
 AWAY = (0, 3, 1, 2)
 
 
-def partial_kernel(meta_ref, rows_ref, own_ref, left_ref, right_ref, train_ref, sum_ref, arrived):
+def partial_kernel(meta_ref, rows_ref, *refs):
+    q_refs, (train_ref, sum_ref, arrived) = refs[:-3], refs[-3:]
     me = meta_ref[0]
     width = train_ref.shape[2]
+    half = sum_ref.shape[1] // 2
     copies = []
     for j, away in enumerate(AWAY):
         columns = pl.ds(pl.multiple_of(((me + away) & 3) * width, width), width)
@@ -164,12 +160,12 @@
             pltpu.make_async_copy(rows_ref.at[:, columns], train_ref.at[j], arrived.at[j])
         )
         copies[-1].start()
-    total = None
-    for j, ref in enumerate((own_ref, left_ref, right_ref)):
-        copies[j].wait()
-        part = dot(train_ref[j], ref[...], ((1,), (1,)))
-        total = part if total is None else total + part
-    sum_ref[...] = total
+    for j, copy in enumerate(copies[:3]):
+        copy.wait()
+        for k in range(2):
+            at = slice(k * half, (k + 1) * half)
+            part = dot(train_ref[j], q_refs[2 * j + k][...], ((1,), (1,)))
+            sum_ref[:, at] = part if j == 0 else sum_ref[:, at] + part
     copies[3].wait()
 
 
@@ -210,11 +206,11 @@
         write(i * TOPK, built)
 
 
-def wide_kernel(meta_ref, train_ref, part_ref, up_ref, down_ref, out_ref, sum_ref, turned_ref):
+def wide_kernel(meta_ref, train_ref, part_ref, far_a_ref, far_b_ref, out_ref, sum_ref, turned_ref):
     half = sum_ref.shape[1] // 2
-    for k, ref in enumerate((up_ref, down_ref)):
+    for k, ref in enumerate((far_a_ref, far_b_ref)):
         at = slice(k * half, (k + 1) * half)
-        sum_ref[:, at] = part_ref[:, at] + dot(train_ref[3], ref[:half, :], ((1,), (1,)))
+        sum_ref[:, at] = part_ref[:, at] + dot(train_ref[3], ref[...], ((1,), (1,)))
 
     def write(at, built):
         out_ref[:, at : at + LANES] = built
@@ -222,15 +218,19 @@
     select(WIDE, meta_ref[1], sum_ref, turned_ref, write)
 
 
+def narrow_partial_kernel(train_ref, own_ref, left_ref, right_ref, sum_ref):
+    total = None
+    for j, ref in enumerate((own_ref, left_ref, right_ref)):
+        part = dot(train_ref[j], ref[...], ((1,), (1,)))
+        total = part if total is None else total + part
+    sum_ref[...] = total
+
+
 def narrow_kernel(
-    meta_ref, train_ref, own_ref, up_ref, down_ref, far_a_ref, far_b_ref, wide_ref, out_ref, sum_ref, turned_ref
+    meta_ref, train_ref, part_ref, far_a_ref, far_b_ref, wide_ref, out_ref, sum_ref, turned_ref
 ):
-    skip = up_ref.shape[0] - sum_ref.shape[1]
     far = jnp.concatenate([far_a_ref[...], far_b_ref[...]], axis=0)
-    blocks = (own_ref[...], up_ref[skip:, :], down_ref[skip:, :], far)
-    sum_ref[...] = functools.reduce(
-        jnp.add, [dot(train_ref[j], q, ((1,), (1,))) for j, q in enumerate(blocks)]
-    )
+    sum_ref[...] = part_ref[...] + dot(train_ref[3], far, ((1,), (1,)))
     done = wide_ref.shape[1]
     out_ref[:, 0, :done] = wide_ref[...]
 
@@ -310,6 +310,15 @@
         scratch_shapes=scratch,
         compiler_params=pltpu.CompilerParams(vmem_limit_bytes=limit),
     )(*operands)
+
+
+def halves(left, right):
+    n = left.shape[0] // 2
+    return left[:n], right[n:]
+
+
+def far(left, right):
+    return shift(left, "tile", 1), shift(right, "tile", -1)
 
 
 def in_hbm(x):
@@ -343,36 +352,36 @@
         ],
     )
     first = exchange_train(first.reshape(sources, WIDE, features))
-    second, first = lax.optimization_barrier((second, first))
+    first = first.reshape(sources * WIDE, features)
+    n = first.shape[0] // 2
+    own_a, own_b = first[:n], first[n:]
+    second, own_a, own_b = lax.optimization_barrier((second, own_a, own_b))
     second = exchange_train(second.reshape(sources, WIDE, features // 2))
-    first = first.reshape(sources * WIDE, features)
-    left, right = near(first)
-    second, left, right = lax.optimization_barrier((second, left, right))
-    doubled = array((2 * sources * NARROW, features), bf16)
-    second, up, down = call(
+    left_a, right_b = shift(own_a, "tile", 1), shift(own_b, "tile", -1)
+    left_a, right_b, own_a, own_b = lax.optimization_barrier((left_a, right_b, own_a, own_b))
+    left_b, right_a = shift(own_b, "tile", 1), shift(own_a, "tile", -1)
+    wide_far = far(left_a, right_b)
+    second, own_a, own_b = lax.optimization_barrier((second, own_a, own_b))
+    second = call(
         unfold_kernel,
-        (array((sources * NARROW, features), bf16), doubled, doubled),
+        array((sources * NARROW, features), bf16),
         second.reshape(sources * WIDE, features // 2),
-        left,
-        right,
-    )
-    after, _ = lax.optimization_barrier((meta, second))
-    up, down = shift(up, "tile", 1), shift(down, "tile", -1)
+    )
+    second_left, second_right = near(second)
     train, part = call(
         partial_kernel,
         (array((4, rows, features), bf16), array((rows, sources * WIDE), f32)),
-        after,
+        meta,
         in_hbm(train_grads),
-        first,
-        left,
-        right,
-        spaces=[SMEM, HBM, VMEM, VMEM, VMEM],
+        own_a,
+        own_b,
+        left_a,
+        left_b,
+        right_a,
+        right_b,
+        spaces=[SMEM, HBM] + [VMEM] * 6,
         scratch=[pltpu.SemaphoreType.DMA((4,))],
     )
-    up, down, part = lax.optimization_barrier((up, down, part))
-    start, middle = sources * NARROW, sources * (NARROW + NARROW // 2)
-    ends = shift(up[start:middle], "tile", 1), shift(down[middle:], "tile", -1)
-
     def room(slots):
         columns = slots * sources
         return [pltpu.VMEM((rows, columns), f32), pltpu.VMEM((columns, LANES), f32)]
@@ -383,22 +392,31 @@
         meta,
         train,
         part,
-        up,
-        down,
+        *wide_far,
         spaces=[SMEM] + [VMEM] * 4,
         scratch=room(WIDE),
     )
+    left, right, wide = lax.optimization_barrier((second_left, second_right, wide))
+    narrow_far = far(*halves(left, right))
+    narrow_part = call(
+        narrow_partial_kernel,
+        array((rows, sources * NARROW), f32),
+        train,
+        second,
+        left,
+        right,
+    )
+
+    wide, narrow_part, *narrow_far = lax.optimization_barrier((wide, narrow_part, *narrow_far))
     both = call(
         narrow_kernel,
         array((sources, 1, (WIDE + NARROW) * TOPK), f32),
         meta,
         train,
-        second,
-        up,
-        down,
-        *ends,
+        narrow_part,
+        *narrow_far,
         wide,
-        spaces=[SMEM] + [VMEM] * 7,
+        spaces=[SMEM] + [VMEM] * 5,
         scratch=room(NARROW),
     )
     both = exchange_train(both)

time: 139 us -> 133 us (0.957)
  blocking collectives: 85.1 us -> 60.8 us
  starting transfers between devices: 9.28 us -> 23.6 us
  waiting for transfers between devices: 20.8 us -> 25.4 us
    all_to_all x3 -> x2, blocking collectives: 85.1 us -> 60.8 us  [exchange_train(): return lax.all_to_all(x, 'train', split_axis=0, concat_axis=0, tiled=True)]
    ppermute x9 -> x13, starting transfers between devices: 9.28 us -> 16.9 us  [shift(): return lax.ppermute(x, axis, [(i, (i + by) % n) for i in range(n)])]
    all_to_all x0 -> x1, starting transfers between devices: none -> 6.74 us  [exchange_train(): return lax.all_to_all(x, 'train', split_axis=0, concat_axis=0, tiled=True)]
    all_to_all x0 -> x1, waiting for transfers between devices: none -> 6.7 us  [exchange_train(): return lax.all_to_all(x, 'train', split_axis=0, concat_axis=0, tiled=True)]
    ppermute x9 -> x13, waiting for transfers between devices: 20.8 us -> 18.7 us  [shift(): return lax.ppermute(x, axis, [(i, (i + by) % n) for i in range(n)])]
    unnamed x14 -> x6, local copies, waits for them, and re-layouts: 3.26 us -> 1.84 us
    pallas_call x7 -> x8, Pallas kernels: 19.8 us -> 20.1 us  [call(): pl.pallas_call(kernel, out_shape=shapes, in_specs=spaces, out_specs=jax.t...]
  transfers between devices with their start and end apart: 9 -> 14, of which waited for: 5 -> 8; matrix products, arithmetic and copies ran while one was open for 0% -> 0% of each run, Pallas kernels for 7% -> 10%
where the time goes in v2:
time: 133 us
  blocking collectives  60.8 us (46%)
  waiting for transfers between devices  25.4 us (19%)
  starting transfers between devices  23.6 us (18%)
  Pallas kernels  20.1 us (15%)
  local copies, waits for them, and re-layouts  1.94 us (1%)
    all_to_all x2, blocking collectives, exchange_train(): return lax.all_to_all(x, 'train', split_axis=0, concat_axis=0, tiled=True)  60.8 us
    pallas_call x8, Pallas kernels, call(): pl.pallas_call(kernel, out_shape=shapes, in_specs=spaces, out_specs=jax.t...  20.1 us
    ppermute x13, waiting for transfers between devices, shift(): return lax.ppermute(x, axis, [(i, (i + by) % n) for i in range(n)])  18.7 us
    ppermute x13, starting transfers between devices, shift(): return lax.ppermute(x, axis, [(i, (i + by) % n) for i in range(n)])  16.9 us
    all_to_all x1, starting transfers between devices, exchange_train(): return lax.all_to_all(x, 'train', split_axis=0, concat_axis=0, tiled=True)  6.74 us
    all_to_all x1, waiting for transfers between devices, exchange_train(): return lax.all_to_all(x, 'train', split_axis=0, concat_axis=0, tiled=True)  6.7 us
  transfers between devices with their start and end apart: 14, of which 8 were waited for; matrix products, arithmetic and copies ran while one was open for 0% of the time, Pallas kernels for 10%

profile of v2, /device:TPU:1, one launch (start us, length us, event | category | flops | bytes accessed | tf_op | source)
XLA Modules:
  0.0 132.8 jit_solution(6397540692260271344)
XLA Ops:
  0.0 3.2 %shard_map.55 = (bf16[512,1024]{1,0:T(8,128)(2,1)S(1)}, bf16[512,512]{1,0:T(8,128)(2,1)}, s32[4,128]{1,0:T(4,128)S(1)}) custom-call(bf16[128,1024]{1,0:T(8,128)(2,1)} %grads_hbm.1, bf16[2,512,512]{2,1,0:T(8,128)(2,1)} %fisher_hbm.1, s32[4,128]{1,0:T(4,128)} %bitcast.15), custom_call_target="tpu_custom_call" | custom-call | tf_op jit(solution)/shard_map/pallas_call | solution.py:305
  3.2 41.5 %all_to_all.15 = bf16[64,8,1024]{2,1,0:T(8,128)(2,1)S(1)} all-to-all(bf16[64,8,1024]{2,1,0:T(8,128)(2,1)S(1)} %bitcast.14), channel_id=1, replica_groups=mesh['train'=64,'tile'=4] {'train'}, dimensions={0} | all-to-all | bytes 2097152 | tf_op jit(solution)/shard_map/all_to_all | solution.py:293
  44.7 0.1 slice_bitcast_fusion
  44.8 1.3 collective-permute-start
  46.1 1.5 %collective-permute-start.1 = (bf16[256,1024]{1,0:T(8,128)(2,1)S(1)}, bf16[256,1024]{1,0:T(8,128)(2,1)}, u32[]{:S(2)}, u32[]{:S(2)}) collective-permute-start(bf16[256,1024]{1,0:T(8,128)(2,1)S(1)} %get-tuple-element.37.refs_1_), channel_id=1, source_target_pairs={{0,3},{1,0},{2,1},{3,2},{4,7},{5,4},{6,5},{7,6},{8,11},{9,8},{10,9... | collective-permute-start | bytes 1572872 | tf_op jit(solution)/shard_map/ppermute | solution.py:289
  47.6 6.7 %all-to-all-start.1 = ((bf16[64,8,512]{2,1,0:T(8,128)(2,1)}), bf16[64,8,512]{2,1,0:T(8,128)(2,1)S(1)}, u32[]{:S(2)}, u32[]{:S(2)}) async-start(bf16[64,8,512]{2,1,0:T(8,128)(2,1)} %bitcast.7), calls=%async_computation.1 | async-start | bytes 1048576 | tf_op jit(solution)/shard_map/all_to_all | solution.py:293
  54.3 5.3 %collective-permute-done.refs_2_ = bf16[256,1024]{1,0:T(8,128)(2,1)S(1)} collective-permute-done((bf16[256,1024]{1,0:T(8,128)(2,1)S(1)}, bf16[256,1024]{1,0:T(8,128)(2,1)S(1)}, u32[]{:S(2)}, u32[]{:S(2)}) %collective-permute-start) | collective-permute-done | bytes 524320 | tf_op jit(solution)/shard_map/ppermute | solution.py:289
  59.6 0.0 collective-permute-done.1.refs_5_
  59.6 1.0 collective-permute-start.2
  60.6 1.7 %collective-permute-start.3 = (bf16[256,1024]{1,0:T(8,128)(2,1)S(1)}, bf16[256,1024]{1,0:T(8,128)(2,1)}, u32[]{:S(2)}, u32[]{:S(2)}) collective-permute-start(bf16[256,1024]{1,0:T(8,128)(2,1)S(1)} %get-tuple-element.36.refs_0_), channel_id=1, source_target_pairs={{0,3},{1,0},{2,1},{3,2},{4,7},{5,4},{6,5},{7,6},{8,11},{9,8},{10,9... | collective-permute-start | bytes 1572872 | tf_op jit(solution)/shard_map/ppermute | solution.py:289
  62.3 0.0 collective-permute-start.6
  62.3 2.7 %collective-permute-start.7 = (bf16[256,1024]{1,0:T(8,128)(2,1)}, bf16[256,1024]{1,0:T(8,128)(2,1)}, u32[]{:S(2)}, u32[]{:S(2)}) collective-permute-start(bf16[256,1024]{1,0:T(8,128)(2,1)} %collective-permute-done.1.refs_5_), channel_id=1, source_target_pairs={{0,3},{1,0},{2,1},{3,2},{4,7},{5,4},{6,5},{7,6},{8,11},{9,8},{10,9... | collective-permute-start | bytes 1572872 | tf_op jit(solution)/shard_map/ppermute | solution.py:289
  64.9 6.7 %all-to-all-done.1 = bf16[64,8,512]{2,1,0:T(8,128)(2,1)S(1)} async-done(((bf16[64,8,512]{2,1,0:T(8,128)(2,1)}), bf16[64,8,512]{2,1,0:T(8,128)(2,1)S(1)}, u32[]{:S(2)}, u32[]{:S(2)}) %all-to-all-start.1) | async-done | bytes 524320 | tf_op jit(solution)/shard_map/all_to_all | solution.py:293
  71.6 0.1 shard_map.57.own_ref
  71.8 0.1 collective-permute-start.4
  71.9 1.4 %collective-permute-done.2.refs_3_ = bf16[256,1024]{1,0:T(8,128)(2,1)S(1)} collective-permute-done((bf16[256,1024]{1,0:T(8,128)(2,1)S(1)}, bf16[256,1024]{1,0:T(8,128)(2,1)S(1)}, u32[]{:S(2)}, u32[]{:S(2)}) %collective-permute-start.2) | collective-permute-done | bytes 524320 | tf_op jit(solution)/shard_map/ppermute | solution.py:289
  73.3 0.0 copy-start
  73.3 0.8 copy-done
  74.1 1.3 collective-permute-start.5
  76.0 0.1 pad_add_fusion.meta_ref
  76.0 0.0 collective-permute-done.3.refs_4_
  76.0 0.0 copy-start.1
  76.1 1.0 copy-done.1
  77.1 6.5 %shard_map.56 = (bf16[4,1024,1024]{2,1,0:T(8,128)(2,1)S(1)}, f32[1024,512]{1,0:T(8,128)S(1)}) custom-call(s32[2]{0:T(128)S(1)} %pad_add_fusion.meta_ref, bf16[1024,4096]{1,0:T(8,128)(2,1)} %rows_ref.1, bf16[256,1024]{1,0:T(8,128)(2,1)S(1)} %get-tuple-element.36.refs_0_, bf16[256,1024]{1,0:T(8,128)(2,1)S(1)} %get-tuple-element.37.refs_1_, ...), custom_call_target="tpu_custom_call" | custom-call | tf_op jit(solution)/shard_map/pallas_call | solution.py:305
  83.6 1.0 collective-permute-done.6.far_a_ref
  84.6 0.0 collective-permute-done.7.far_b_ref
  84.6 4.6 %shard_map.58.wide_ref = f32[64,256]{1,0:T(8,128)S(1)} custom-call(s32[2]{0:T(128)S(1)} %pad_add_fusion.meta_ref, bf16[4,1024,1024]{2,1,0:T(8,128)(2,1)S(1)} %get-tuple-element.40.train_ref, f32[1024,512]{1,0:T(8,128)S(1)} %get-tuple-element.42.part_ref, bf16[256,1024]{1,0:T(8,128)(2,1)} %collective-permute-done.6.far_a_ref, ...), custom_call_target="tpu_custom_call" | custom-call | tf_op jit(solution)/shard_map/pallas_call | solution.py:305
  89.3 6.5 %collective-permute-done.4.left_ref = bf16[256,1024]{1,0:T(8,128)(2,1)S(1)} collective-permute-done((bf16[256,1024]{1,0:T(8,128)(2,1)S(1)}, bf16[256,1024]{1,0:T(8,128)(2,1)S(1)}, u32[]{:S(2)}, u32[]{:S(2)}) %collective-permute-start.4) | collective-permute-done | bytes 524320 | tf_op jit(solution)/shard_map/ppermute | solution.py:289
  95.7 0.0 collective-permute-done.5.right_ref
  95.8 0.3 collective-permute-start.8
  96.1 0.0 copy-start.2
  96.1 2.6 %collective-permute-start.9 = (bf16[128,1024]{1,0:T(8,128)(2,1)S(1)}, bf16[128,1024]{1,0:T(8,128)(2,1)S(1)}, u32[]{:S(2)}, u32[]{:S(2)}) collective-permute-start(bf16[128,1024]{1,0:T(8,128)(2,1)S(1)} %slice.23), channel_id=1, source_target_pairs={{0,3},{1,0},{2,1},{3,2},{4,7},{5,4},{6,5},{7,6},{8,11},{9,8},{10,9... | collective-permute-start | bytes 786440 | tf_op jit(solution)/shard_map/ppermute | solution.py:289
  98.6 1.8 %shard_map.59.part_ref = f32[1024,256]{1,0:T(8,128)S(1)} custom-call(bf16[4,1024,1024]{2,1,0:T(8,128)(2,1)S(1)} %get-tuple-element.40.train_ref, bf16[256,1024]{1,0:T(8,128)(2,1)S(1)} %shard_map.57.own_ref, bf16[256,1024]{1,0:T(8,128)(2,1)S(1)} %collective-permute-done.4.left_ref, bf16[256,1024]{1,0:T(8,128)(2,1)S(1)} %collective-permute-done.5.right_ref), custom_call_target="tpu_custom_call" | custom-call | tf_op jit(solution)/shard_map/pallas_call | solution.py:305
  100.5 2.5 %collective-permute-done.8.far_a_ref = bf16[128,1024]{1,0:T(8,128)(2,1)S(1)} collective-permute-done((bf16[128,1024]{1,0:T(8,128)(2,1)S(1)}, bf16[128,1024]{1,0:T(8,128)(2,1)S(1)}, u32[]{:S(2)}, u32[]{:S(2)}) %collective-permute-start.8) | collective-permute-done | bytes 262176 | tf_op jit(solution)/shard_map/ppermute | solution.py:289
  103.0 0.0 collective-permute-done.9.far_b_ref
  103.0 2.4 %shard_map.60 = f32[64,1,384]{2,1,0:T(1,128)S(1)} custom-call(s32[2]{0:T(128)S(1)} %pad_add_fusion.meta_ref, bf16[4,1024,1024]{2,1,0:T(8,128)(2,1)S(1)} %get-tuple-element.40.train_ref, f32[1024,256]{1,0:T(8,128)S(1)} %shard_map.59.part_ref, bf16[128,1024]{1,0:T(8,128)(2,1)S(1)} %collective-permute-done.8.far_a_ref, ...), custom_call_target="tpu_custom_call" | custom-call | tf_op jit(solution)/shard_map/pallas_call | solution.py:305
  105.3 19.3 %all_to_all.16.returned_ref = f32[64,1,384]{2,1,0:T(1,128)S(1)} all-to-all(f32[64,1,384]{2,1,0:T(1,128)S(1)} %shard_map.60), channel_id=1, replica_groups=mesh['train'=64,'tile'=4] {'train'}, dimensions={0} | all-to-all | bytes 196608 | tf_op jit(solution)/shard_map/all_to_all | solution.py:293
  124.7 0.0 copy-done.2
  124.7 0.8 shard_map.61
  125.5 0.7 collective-permute-start.10
  126.2 3.3 %collective-permute-start.11 = (f32[32,128]{1,0:T(8,128)S(1)}, f32[32,128]{1,0:T(8,128)S(1)}, u32[]{:S(2)}, u32[]{:S(2)}) collective-permute-start(f32[32,128]{1,0:T(8,128)S(1)} %get-tuple-element.51.a_ref), channel_id=1, source_target_pairs={{0,2},{1,3},{2,0},{3,1},{4,6},{5,7},{6,4},{7,5},{8,10},{9,11},{10,... | collective-permute-start | bytes 49160 | tf_op jit(solution)/shard_map/ppermute | solution.py:289
  129.6 0.5 collective-permute-start.12
  130.1 0.0 collective-permute-done.10.b_ref
  130.1 0.8 collective-permute-done.11.c_ref
  130.9 1.3 collective-permute-done.12.d_ref
  132.1 0.6 shard_map.62
  (2 shorter events, 0.0 us)
Async XLA Ops:
  44.8 14.8 %collective-permute-start = (bf16[256,1024]{1,0:T(8,128)(2,1)S(1)}, bf16[256,1024]{1,0:T(8,128)(2,1)S(1)}, u32[]{:S(2)}, u32[]{:S(2)}) collective-permute-start(bf16[256,1024]{1,0:T(8,128)(2,1)S(1)} %get-tuple-element.36.refs_0_), channel_id=1, source_target_pairs={{0,1},{1,2},{2,3},{3,0},{4,5},{5,6},{6,7},{7,4},{8,9},{9,10},{10,1... | collective-permute-start | bytes 1572872 | tf_op jit(solution)/shard_map/ppermute | solution.py:289
  46.1 13.5 %collective-permute-start.1 = (bf16[256,1024]{1,0:T(8,128)(2,1)S(1)}, bf16[256,1024]{1,0:T(8,128)(2,1)}, u32[]{:S(2)}, u32[]{:S(2)}) collective-permute-start(bf16[256,1024]{1,0:T(8,128)(2,1)S(1)} %get-tuple-element.37.refs_1_), channel_id=1, source_target_pairs={{0,3},{1,0},{2,1},{3,2},{4,7},{5,4},{6,5},{7,6},{8,11},{9,8},{10,9... | collective-permute-start | bytes 1572872 | tf_op jit(solution)/shard_map/ppermute | solution.py:289
  47.6 24.1 %all-to-all-start.1 = ((bf16[64,8,512]{2,1,0:T(8,128)(2,1)}), bf16[64,8,512]{2,1,0:T(8,128)(2,1)S(1)}, u32[]{:S(2)}, u32[]{:S(2)}) async-start(bf16[64,8,512]{2,1,0:T(8,128)(2,1)} %bitcast.7), calls=%async_computation.1 | async-start | bytes 1048576 | tf_op jit(solution)/shard_map/all_to_all | solution.py:293
  59.6 13.7 %collective-permute-start.2 = (bf16[256,1024]{1,0:T(8,128)(2,1)S(1)}, bf16[256,1024]{1,0:T(8,128)(2,1)S(1)}, u32[]{:S(2)}, u32[]{:S(2)}) collective-permute-start(bf16[256,1024]{1,0:T(8,128)(2,1)S(1)} %get-tuple-element.37.refs_1_), channel_id=1, source_target_pairs={{0,1},{1,2},{2,3},{3,0},{4,5},{5,6},{6,7},{7,4},{8,9},{9,10},{10,1... | collective-permute-start | bytes 1572872 | tf_op jit(solution)/shard_map/ppermute | solution.py:289
  60.6 15.5 %collective-permute-start.3 = (bf16[256,1024]{1,0:T(8,128)(2,1)S(1)}, bf16[256,1024]{1,0:T(8,128)(2,1)}, u32[]{:S(2)}, u32[]{:S(2)}) collective-permute-start(bf16[256,1024]{1,0:T(8,128)(2,1)S(1)} %get-tuple-element.36.refs_0_), channel_id=1, source_target_pairs={{0,3},{1,0},{2,1},{3,2},{4,7},{5,4},{6,5},{7,6},{8,11},{9,8},{10,9... | collective-permute-start | bytes 1572872 | tf_op jit(solution)/shard_map/ppermute | solution.py:289
  62.3 22.3 %collective-permute-start.6 = (bf16[256,1024]{1,0:T(8,128)(2,1)S(1)}, bf16[256,1024]{1,0:T(8,128)(2,1)}, u32[]{:S(2)}, u32[]{:S(2)}) collective-permute-start(bf16[256,1024]{1,0:T(8,128)(2,1)S(1)} %collective-permute-done.refs_2_), channel_id=1, source_target_pairs={{0,1},{1,2},{2,3},{3,0},{4,5},{5,6},{6,7},{7,4},{8,9},{9,10},{10,1... | collective-permute-start | bytes 1572872 | tf_op jit(solution)/shard_map/ppermute | solution.py:289
  62.3 22.3 %collective-permute-start.7 = (bf16[256,1024]{1,0:T(8,128)(2,1)}, bf16[256,1024]{1,0:T(8,128)(2,1)}, u32[]{:S(2)}, u32[]{:S(2)}) collective-permute-start(bf16[256,1024]{1,0:T(8,128)(2,1)} %collective-permute-done.1.refs_5_), channel_id=1, source_target_pairs={{0,3},{1,0},{2,1},{3,2},{4,7},{5,4},{6,5},{7,6},{8,11},{9,8},{10,9... | collective-permute-start | bytes 1572872 | tf_op jit(solution)/shard_map/ppermute | solution.py:289
  71.8 24.0 %collective-permute-start.4 = (bf16[256,1024]{1,0:T(8,128)(2,1)S(1)}, bf16[256,1024]{1,0:T(8,128)(2,1)S(1)}, u32[]{:S(2)}, u32[]{:S(2)}) collective-permute-start(bf16[256,1024]{1,0:T(8,128)(2,1)S(1)} %shard_map.57.own_ref), channel_id=1, source_target_pairs={{0,1},{1,2},{2,3},{3,0},{4,5},{5,6},{6,7},{7,4},{8,9},{9,10},{10,1... | collective-permute-start | bytes 1572872 | tf_op jit(solution)/shard_map/ppermute | solution.py:289
  73.3 0.8 copy-start
  74.1 21.7 %collective-permute-start.5 = (bf16[256,1024]{1,0:T(8,128)(2,1)S(1)}, bf16[256,1024]{1,0:T(8,128)(2,1)S(1)}, u32[]{:S(2)}, u32[]{:S(2)}) collective-permute-start(bf16[256,1024]{1,0:T(8,128)(2,1)S(1)} %shard_map.57.own_ref), channel_id=1, source_target_pairs={{0,3},{1,0},{2,1},{3,2},{4,7},{5,4},{6,5},{7,6},{8,11},{9,8},{10,9... | collective-permute-start | bytes 1572872 | tf_op jit(solution)/shard_map/ppermute | solution.py:289
  76.0 1.0 copy-start.1
  95.8 7.2 %collective-permute-start.8 = (bf16[128,1024]{1,0:T(8,128)(2,1)S(1)}, bf16[128,1024]{1,0:T(8,128)(2,1)S(1)}, u32[]{:S(2)}, u32[]{:S(2)}) collective-permute-start(bf16[128,1024]{1,0:T(8,128)(2,1)S(1)} %slice.22), channel_id=1, source_target_pairs={{0,1},{1,2},{2,3},{3,0},{4,5},{5,6},{6,7},{7,4},{8,9},{9,10},{10,1... | collective-permute-start | bytes 786440 | tf_op jit(solution)/shard_map/ppermute | solution.py:289
  96.1 28.6 %copy-start.2 = (s32[128,4]{0,1:T(4,128)S(1)}, s32[128,4]{0,1:T(4,128)}, u32[]{:S(2)}) copy-start(s32[128,4]{0,1:T(4,128)} %param.8) | copy-start | bytes 6148
  96.1 6.9 %collective-permute-start.9 = (bf16[128,1024]{1,0:T(8,128)(2,1)S(1)}, bf16[128,1024]{1,0:T(8,128)(2,1)S(1)}, u32[]{:S(2)}, u32[]{:S(2)}) collective-permute-start(bf16[128,1024]{1,0:T(8,128)(2,1)S(1)} %slice.23), channel_id=1, source_target_pairs={{0,3},{1,0},{2,1},{3,2},{4,7},{5,4},{6,5},{7,6},{8,11},{9,8},{10,9... | collective-permute-start | bytes 786440 | tf_op jit(solution)/shard_map/ppermute | solution.py:289
  125.5 4.6 %collective-permute-start.10 = (f32[32,128]{1,0:T(8,128)S(1)}, f32[32,128]{1,0:T(8,128)S(1)}, u32[]{:S(2)}, u32[]{:S(2)}) collective-permute-start(f32[32,128]{1,0:T(8,128)S(1)} %get-tuple-element.52), channel_id=1, source_target_pairs={{0,1},{1,2},{2,3},{3,0},{4,5},{5,6},{6,7},{7,4},{8,9},{9,10},{10,1... | collective-permute-start | bytes 49160 | tf_op jit(solution)/shard_map/ppermute | solution.py:289
  126.2 4.6 %collective-permute-start.11 = (f32[32,128]{1,0:T(8,128)S(1)}, f32[32,128]{1,0:T(8,128)S(1)}, u32[]{:S(2)}, u32[]{:S(2)}) collective-permute-start(f32[32,128]{1,0:T(8,128)S(1)} %get-tuple-element.51.a_ref), channel_id=1, source_target_pairs={{0,2},{1,3},{2,0},{3,1},{4,6},{5,7},{6,4},{7,5},{8,10},{9,11},{10,... | collective-permute-start | bytes 49160 | tf_op jit(solution)/shard_map/ppermute | solution.py:289
  129.6 2.6 %collective-permute-start.12 = (f32[32,128]{1,0:T(8,128)S(1)}, f32[32,128]{1,0:T(8,128)S(1)}, u32[]{:S(2)}, u32[]{:S(2)}) collective-permute-start(f32[32,128]{1,0:T(8,128)S(1)} %get-tuple-element.52), channel_id=1, source_target_pairs={{0,3},{1,0},{2,1},{3,2},{4,7},{5,4},{6,5},{7,6},{8,11},{9,8},{10,9... | collective-permute-start | bytes 49160 | tf_op jit(solution)/shard_map/ppermute | solution.py:289

commit v3 on v2

--- a/solution.py
+++ b/solution.py
@@ -384,7 +384,8 @@
     )
     def room(slots):
         columns = slots * sources
-        return [pltpu.VMEM((rows, columns), f32), pltpu.VMEM((columns, LANES), f32)]
+        turned = pltpu.VMEM((columns + SUBLANES, LANES), f32)
+        return [pltpu.VMEM((rows, columns), f32), turned]
 
     wide = call(
         wide_kernel,

time: 133 us -> 133 us (level)
  no operation moved by 1% of the time
where the time goes in v3:
time: 133 us
  blocking collectives  60.8 us (46%)
  waiting for transfers between devices  25.4 us (19%)
  starting transfers between devices  23.6 us (18%)
  Pallas kernels  20.1 us (15%)
  local copies, waits for them, and re-layouts  1.94 us (1%)
    all_to_all x2, blocking collectives, exchange_train(): return lax.all_to_all(x, 'train', split_axis=0, concat_axis=0, tiled=True)  60.8 us
    pallas_call x8, Pallas kernels, call(): pl.pallas_call(kernel, out_shape=shapes, in_specs=spaces, out_specs=jax.t...  20.1 us
    ppermute x13, waiting for transfers between devices, shift(): return lax.ppermute(x, axis, [(i, (i + by) % n) for i in range(n)])  18.7 us
    ppermute x13, starting transfers between devices, shift(): return lax.ppermute(x, axis, [(i, (i + by) % n) for i in range(n)])  16.9 us
    all_to_all x1, starting transfers between devices, exchange_train(): return lax.all_to_all(x, 'train', split_axis=0, concat_axis=0, tiled=True)  6.74 us
    all_to_all x1, waiting for transfers between devices, exchange_train(): return lax.all_to_all(x, 'train', split_axis=0, concat_axis=0, tiled=True)  6.7 us
  transfers between devices with their start and end apart: 14, of which 8 were waited for; matrix products, arithmetic and copies ran while one was open for 0% of the time, Pallas kernels for 10%

profile of v3, /device:TPU:1, one launch (start us, length us, event | category | flops | bytes accessed | tf_op | source)
XLA Modules:
  0.0 132.8 jit_solution(759405786591891090)
XLA Ops:
  0.0 3.2 %shard_map.55 = (bf16[512,1024]{1,0:T(8,128)(2,1)S(1)}, bf16[512,512]{1,0:T(8,128)(2,1)}, s32[4,128]{1,0:T(4,128)S(1)}) custom-call(bf16[128,1024]{1,0:T(8,128)(2,1)} %grads_hbm.1, bf16[2,512,512]{2,1,0:T(8,128)(2,1)} %fisher_hbm.1, s32[4,128]{1,0:T(4,128)} %bitcast.15), custom_call_target="tpu_custom_call" | custom-call | tf_op jit(solution)/shard_map/pallas_call | solution.py:305
  3.2 41.5 %all_to_all.15 = bf16[64,8,1024]{2,1,0:T(8,128)(2,1)S(1)} all-to-all(bf16[64,8,1024]{2,1,0:T(8,128)(2,1)S(1)} %bitcast.14), channel_id=1, replica_groups=mesh['train'=64,'tile'=4] {'train'}, dimensions={0} | all-to-all | bytes 2097152 | tf_op jit(solution)/shard_map/all_to_all | solution.py:293
  44.7 0.1 slice_bitcast_fusion
  44.8 1.3 collective-permute-start
  46.1 1.5 %collective-permute-start.1 = (bf16[256,1024]{1,0:T(8,128)(2,1)S(1)}, bf16[256,1024]{1,0:T(8,128)(2,1)}, u32[]{:S(2)}, u32[]{:S(2)}) collective-permute-start(bf16[256,1024]{1,0:T(8,128)(2,1)S(1)} %get-tuple-element.37.refs_1_), channel_id=1, source_target_pairs={{0,3},{1,0},{2,1},{3,2},{4,7},{5,4},{6,5},{7,6},{8,11},{9,8},{10,9... | collective-permute-start | bytes 1572872 | tf_op jit(solution)/shard_map/ppermute | solution.py:289
  47.6 6.7 %all-to-all-start.1 = ((bf16[64,8,512]{2,1,0:T(8,128)(2,1)}), bf16[64,8,512]{2,1,0:T(8,128)(2,1)S(1)}, u32[]{:S(2)}, u32[]{:S(2)}) async-start(bf16[64,8,512]{2,1,0:T(8,128)(2,1)} %bitcast.7), calls=%async_computation.1 | async-start | bytes 1048576 | tf_op jit(solution)/shard_map/all_to_all | solution.py:293
  54.3 5.3 %collective-permute-done.refs_2_ = bf16[256,1024]{1,0:T(8,128)(2,1)S(1)} collective-permute-done((bf16[256,1024]{1,0:T(8,128)(2,1)S(1)}, bf16[256,1024]{1,0:T(8,128)(2,1)S(1)}, u32[]{:S(2)}, u32[]{:S(2)}) %collective-permute-start) | collective-permute-done | bytes 524320 | tf_op jit(solution)/shard_map/ppermute | solution.py:289
  59.6 0.0 collective-permute-done.1.refs_5_
  59.6 1.0 collective-permute-start.2
  60.6 1.7 %collective-permute-start.3 = (bf16[256,1024]{1,0:T(8,128)(2,1)S(1)}, bf16[256,1024]{1,0:T(8,128)(2,1)}, u32[]{:S(2)}, u32[]{:S(2)}) collective-permute-start(bf16[256,1024]{1,0:T(8,128)(2,1)S(1)} %get-tuple-element.36.refs_0_), channel_id=1, source_target_pairs={{0,3},{1,0},{2,1},{3,2},{4,7},{5,4},{6,5},{7,6},{8,11},{9,8},{10,9... | collective-permute-start | bytes 1572872 | tf_op jit(solution)/shard_map/ppermute | solution.py:289
  62.3 0.0 collective-permute-start.6
  62.3 2.7 %collective-permute-start.7 = (bf16[256,1024]{1,0:T(8,128)(2,1)}, bf16[256,1024]{1,0:T(8,128)(2,1)}, u32[]{:S(2)}, u32[]{:S(2)}) collective-permute-start(bf16[256,1024]{1,0:T(8,128)(2,1)} %collective-permute-done.1.refs_5_), channel_id=1, source_target_pairs={{0,3},{1,0},{2,1},{3,2},{4,7},{5,4},{6,5},{7,6},{8,11},{9,8},{10,9... | collective-permute-start | bytes 1572872 | tf_op jit(solution)/shard_map/ppermute | solution.py:289
  64.9 6.7 %all-to-all-done.1 = bf16[64,8,512]{2,1,0:T(8,128)(2,1)S(1)} async-done(((bf16[64,8,512]{2,1,0:T(8,128)(2,1)}), bf16[64,8,512]{2,1,0:T(8,128)(2,1)S(1)}, u32[]{:S(2)}, u32[]{:S(2)}) %all-to-all-start.1) | async-done | bytes 524320 | tf_op jit(solution)/shard_map/all_to_all | solution.py:293
  71.6 0.1 shard_map.57.own_ref
  71.8 0.1 collective-permute-start.4
  71.9 1.4 %collective-permute-done.2.refs_3_ = bf16[256,1024]{1,0:T(8,128)(2,1)S(1)} collective-permute-done((bf16[256,1024]{1,0:T(8,128)(2,1)S(1)}, bf16[256,1024]{1,0:T(8,128)(2,1)S(1)}, u32[]{:S(2)}, u32[]{:S(2)}) %collective-permute-start.2) | collective-permute-done | bytes 524320 | tf_op jit(solution)/shard_map/ppermute | solution.py:289
  73.3 0.0 copy-start
  73.3 0.8 copy-done
  74.1 1.3 collective-permute-start.5
  76.0 0.1 pad_add_fusion.meta_ref
  76.0 0.0 collective-permute-done.3.refs_4_
  76.0 0.0 copy-start.1
  76.1 1.0 copy-done.1
  77.1 6.5 %shard_map.56 = (bf16[4,1024,1024]{2,1,0:T(8,128)(2,1)S(1)}, f32[1024,512]{1,0:T(8,128)S(1)}) custom-call(s32[2]{0:T(128)S(1)} %pad_add_fusion.meta_ref, bf16[1024,4096]{1,0:T(8,128)(2,1)} %rows_ref.1, bf16[256,1024]{1,0:T(8,128)(2,1)S(1)} %get-tuple-element.36.refs_0_, bf16[256,1024]{1,0:T(8,128)(2,1)S(1)} %get-tuple-element.37.refs_1_, ...), custom_call_target="tpu_custom_call" | custom-call | tf_op jit(solution)/shard_map/pallas_call | solution.py:305
  83.6 1.0 collective-permute-done.6.far_a_ref
  84.6 0.0 collective-permute-done.7.far_b_ref
  84.6 4.6 %shard_map.58.wide_ref = f32[64,256]{1,0:T(8,128)S(1)} custom-call(s32[2]{0:T(128)S(1)} %pad_add_fusion.meta_ref, bf16[4,1024,1024]{2,1,0:T(8,128)(2,1)S(1)} %get-tuple-element.40.train_ref, f32[1024,512]{1,0:T(8,128)S(1)} %get-tuple-element.42.part_ref, bf16[256,1024]{1,0:T(8,128)(2,1)} %collective-permute-done.6.far_a_ref, ...), custom_call_target="tpu_custom_call" | custom-call | tf_op jit(solution)/shard_map/pallas_call | solution.py:305
  89.3 6.5 %collective-permute-done.4.left_ref = bf16[256,1024]{1,0:T(8,128)(2,1)S(1)} collective-permute-done((bf16[256,1024]{1,0:T(8,128)(2,1)S(1)}, bf16[256,1024]{1,0:T(8,128)(2,1)S(1)}, u32[]{:S(2)}, u32[]{:S(2)}) %collective-permute-start.4) | collective-permute-done | bytes 524320 | tf_op jit(solution)/shard_map/ppermute | solution.py:289
  95.7 0.0 collective-permute-done.5.right_ref
  95.8 0.3 collective-permute-start.8
  96.1 0.0 copy-start.2
  96.1 2.6 %collective-permute-start.9 = (bf16[128,1024]{1,0:T(8,128)(2,1)S(1)}, bf16[128,1024]{1,0:T(8,128)(2,1)S(1)}, u32[]{:S(2)}, u32[]{:S(2)}) collective-permute-start(bf16[128,1024]{1,0:T(8,128)(2,1)S(1)} %slice.23), channel_id=1, source_target_pairs={{0,3},{1,0},{2,1},{3,2},{4,7},{5,4},{6,5},{7,6},{8,11},{9,8},{10,9... | collective-permute-start | bytes 786440 | tf_op jit(solution)/shard_map/ppermute | solution.py:289
  98.6 1.8 %shard_map.59.part_ref = f32[1024,256]{1,0:T(8,128)S(1)} custom-call(bf16[4,1024,1024]{2,1,0:T(8,128)(2,1)S(1)} %get-tuple-element.40.train_ref, bf16[256,1024]{1,0:T(8,128)(2,1)S(1)} %shard_map.57.own_ref, bf16[256,1024]{1,0:T(8,128)(2,1)S(1)} %collective-permute-done.4.left_ref, bf16[256,1024]{1,0:T(8,128)(2,1)S(1)} %collective-permute-done.5.right_ref), custom_call_target="tpu_custom_call" | custom-call | tf_op jit(solution)/shard_map/pallas_call | solution.py:305
  100.5 2.5 %collective-permute-done.8.far_a_ref = bf16[128,1024]{1,0:T(8,128)(2,1)S(1)} collective-permute-done((bf16[128,1024]{1,0:T(8,128)(2,1)S(1)}, bf16[128,1024]{1,0:T(8,128)(2,1)S(1)}, u32[]{:S(2)}, u32[]{:S(2)}) %collective-permute-start.8) | collective-permute-done | bytes 262176 | tf_op jit(solution)/shard_map/ppermute | solution.py:289
  103.0 0.0 collective-permute-done.9.far_b_ref
  103.0 2.4 %shard_map.60 = f32[64,1,384]{2,1,0:T(1,128)S(1)} custom-call(s32[2]{0:T(128)S(1)} %pad_add_fusion.meta_ref, bf16[4,1024,1024]{2,1,0:T(8,128)(2,1)S(1)} %get-tuple-element.40.train_ref, f32[1024,256]{1,0:T(8,128)S(1)} %shard_map.59.part_ref, bf16[128,1024]{1,0:T(8,128)(2,1)S(1)} %collective-permute-done.8.far_a_ref, ...), custom_call_target="tpu_custom_call" | custom-call | tf_op jit(solution)/shard_map/pallas_call | solution.py:305
  105.3 19.3 %all_to_all.16.returned_ref = f32[64,1,384]{2,1,0:T(1,128)S(1)} all-to-all(f32[64,1,384]{2,1,0:T(1,128)S(1)} %shard_map.60), channel_id=1, replica_groups=mesh['train'=64,'tile'=4] {'train'}, dimensions={0} | all-to-all | bytes 196608 | tf_op jit(solution)/shard_map/all_to_all | solution.py:293
  124.7 0.0 copy-done.2
  124.7 0.8 shard_map.61
  125.5 0.7 collective-permute-start.10
  126.2 3.3 %collective-permute-start.11 = (f32[32,128]{1,0:T(8,128)S(1)}, f32[32,128]{1,0:T(8,128)S(1)}, u32[]{:S(2)}, u32[]{:S(2)}) collective-permute-start(f32[32,128]{1,0:T(8,128)S(1)} %get-tuple-element.51.a_ref), channel_id=1, source_target_pairs={{0,2},{1,3},{2,0},{3,1},{4,6},{5,7},{6,4},{7,5},{8,10},{9,11},{10,... | collective-permute-start | bytes 49160 | tf_op jit(solution)/shard_map/ppermute | solution.py:289
  129.6 0.5 collective-permute-start.12
  130.1 0.0 collective-permute-done.10.b_ref
  130.1 0.8 collective-permute-done.11.c_ref
  130.9 1.3 collective-permute-done.12.d_ref
  132.1 0.6 shard_map.62
  (2 shorter events, 0.0 us)
Async XLA Ops:
  44.8 14.8 %collective-permute-start = (bf16[256,1024]{1,0:T(8,128)(2,1)S(1)}, bf16[256,1024]{1,0:T(8,128)(2,1)S(1)}, u32[]{:S(2)}, u32[]{:S(2)}) collective-permute-start(bf16[256,1024]{1,0:T(8,128)(2,1)S(1)} %get-tuple-element.36.refs_0_), channel_id=1, source_target_pairs={{0,1},{1,2},{2,3},{3,0},{4,5},{5,6},{6,7},{7,4},{8,9},{9,10},{10,1... | collective-permute-start | bytes 1572872 | tf_op jit(solution)/shard_map/ppermute | solution.py:289
  46.1 13.5 %collective-permute-start.1 = (bf16[256,1024]{1,0:T(8,128)(2,1)S(1)}, bf16[256,1024]{1,0:T(8,128)(2,1)}, u32[]{:S(2)}, u32[]{:S(2)}) collective-permute-start(bf16[256,1024]{1,0:T(8,128)(2,1)S(1)} %get-tuple-element.37.refs_1_), channel_id=1, source_target_pairs={{0,3},{1,0},{2,1},{3,2},{4,7},{5,4},{6,5},{7,6},{8,11},{9,8},{10,9... | collective-permute-start | bytes 1572872 | tf_op jit(solution)/shard_map/ppermute | solution.py:289
  47.6 24.1 %all-to-all-start.1 = ((bf16[64,8,512]{2,1,0:T(8,128)(2,1)}), bf16[64,8,512]{2,1,0:T(8,128)(2,1)S(1)}, u32[]{:S(2)}, u32[]{:S(2)}) async-start(bf16[64,8,512]{2,1,0:T(8,128)(2,1)} %bitcast.7), calls=%async_computation.1 | async-start | bytes 1048576 | tf_op jit(solution)/shard_map/all_to_all | solution.py:293
  59.6 13.7 %collective-permute-start.2 = (bf16[256,1024]{1,0:T(8,128)(2,1)S(1)}, bf16[256,1024]{1,0:T(8,128)(2,1)S(1)}, u32[]{:S(2)}, u32[]{:S(2)}) collective-permute-start(bf16[256,1024]{1,0:T(8,128)(2,1)S(1)} %get-tuple-element.37.refs_1_), channel_id=1, source_target_pairs={{0,1},{1,2},{2,3},{3,0},{4,5},{5,6},{6,7},{7,4},{8,9},{9,10},{10,1... | collective-permute-start | bytes 1572872 | tf_op jit(solution)/shard_map/ppermute | solution.py:289
  60.6 15.5 %collective-permute-start.3 = (bf16[256,1024]{1,0:T(8,128)(2,1)S(1)}, bf16[256,1024]{1,0:T(8,128)(2,1)}, u32[]{:S(2)}, u32[]{:S(2)}) collective-permute-start(bf16[256,1024]{1,0:T(8,128)(2,1)S(1)} %get-tuple-element.36.refs_0_), channel_id=1, source_target_pairs={{0,3},{1,0},{2,1},{3,2},{4,7},{5,4},{6,5},{7,6},{8,11},{9,8},{10,9... | collective-permute-start | bytes 1572872 | tf_op jit(solution)/shard_map/ppermute | solution.py:289
  62.3 22.3 %collective-permute-start.6 = (bf16[256,1024]{1,0:T(8,128)(2,1)S(1)}, bf16[256,1024]{1,0:T(8,128)(2,1)}, u32[]{:S(2)}, u32[]{:S(2)}) collective-permute-start(bf16[256,1024]{1,0:T(8,128)(2,1)S(1)} %collective-permute-done.refs_2_), channel_id=1, source_target_pairs={{0,1},{1,2},{2,3},{3,0},{4,5},{5,6},{6,7},{7,4},{8,9},{9,10},{10,1... | collective-permute-start | bytes 1572872 | tf_op jit(solution)/shard_map/ppermute | solution.py:289
  62.3 22.3 %collective-permute-start.7 = (bf16[256,1024]{1,0:T(8,128)(2,1)}, bf16[256,1024]{1,0:T(8,128)(2,1)}, u32[]{:S(2)}, u32[]{:S(2)}) collective-permute-start(bf16[256,1024]{1,0:T(8,128)(2,1)} %collective-permute-done.1.refs_5_), channel_id=1, source_target_pairs={{0,3},{1,0},{2,1},{3,2},{4,7},{5,4},{6,5},{7,6},{8,11},{9,8},{10,9... | collective-permute-start | bytes 1572872 | tf_op jit(solution)/shard_map/ppermute | solution.py:289
  71.8 24.0 %collective-permute-start.4 = (bf16[256,1024]{1,0:T(8,128)(2,1)S(1)}, bf16[256,1024]{1,0:T(8,128)(2,1)S(1)}, u32[]{:S(2)}, u32[]{:S(2)}) collective-permute-start(bf16[256,1024]{1,0:T(8,128)(2,1)S(1)} %shard_map.57.own_ref), channel_id=1, source_target_pairs={{0,1},{1,2},{2,3},{3,0},{4,5},{5,6},{6,7},{7,4},{8,9},{9,10},{10,1... | collective-permute-start | bytes 1572872 | tf_op jit(solution)/shard_map/ppermute | solution.py:289
  73.3 0.8 copy-start
  74.1 21.7 %collective-permute-start.5 = (bf16[256,1024]{1,0:T(8,128)(2,1)S(1)}, bf16[256,1024]{1,0:T(8,128)(2,1)S(1)}, u32[]{:S(2)}, u32[]{:S(2)}) collective-permute-start(bf16[256,1024]{1,0:T(8,128)(2,1)S(1)} %shard_map.57.own_ref), channel_id=1, source_target_pairs={{0,3},{1,0},{2,1},{3,2},{4,7},{5,4},{6,5},{7,6},{8,11},{9,8},{10,9... | collective-permute-start | bytes 1572872 | tf_op jit(solution)/shard_map/ppermute | solution.py:289
  76.0 1.0 copy-start.1
  95.8 7.2 %collective-permute-start.8 = (bf16[128,1024]{1,0:T(8,128)(2,1)S(1)}, bf16[128,1024]{1,0:T(8,128)(2,1)S(1)}, u32[]{:S(2)}, u32[]{:S(2)}) collective-permute-start(bf16[128,1024]{1,0:T(8,128)(2,1)S(1)} %slice.22), channel_id=1, source_target_pairs={{0,1},{1,2},{2,3},{3,0},{4,5},{5,6},{6,7},{7,4},{8,9},{9,10},{10,1... | collective-permute-start | bytes 786440 | tf_op jit(solution)/shard_map/ppermute | solution.py:289
  96.1 28.6 %copy-start.2 = (s32[128,4]{0,1:T(4,128)S(1)}, s32[128,4]{0,1:T(4,128)}, u32[]{:S(2)}) copy-start(s32[128,4]{0,1:T(4,128)} %param.8) | copy-start | bytes 6148
  96.1 6.9 %collective-permute-start.9 = (bf16[128,1024]{1,0:T(8,128)(2,1)S(1)}, bf16[128,1024]{1,0:T(8,128)(2,1)S(1)}, u32[]{:S(2)}, u32[]{:S(2)}) collective-permute-start(bf16[128,1024]{1,0:T(8,128)(2,1)S(1)} %slice.23), channel_id=1, source_target_pairs={{0,3},{1,0},{2,1},{3,2},{4,7},{5,4},{6,5},{7,6},{8,11},{9,8},{10,9... | collective-permute-start | bytes 786440 | tf_op jit(solution)/shard_map/ppermute | solution.py:289
  125.5 4.6 %collective-permute-start.10 = (f32[32,128]{1,0:T(8,128)S(1)}, f32[32,128]{1,0:T(8,128)S(1)}, u32[]{:S(2)}, u32[]{:S(2)}) collective-permute-start(f32[32,128]{1,0:T(8,128)S(1)} %get-tuple-element.52), channel_id=1, source_target_pairs={{0,1},{1,2},{2,3},{3,0},{4,5},{5,6},{6,7},{7,4},{8,9},{9,10},{10,1... | collective-permute-start | bytes 49160 | tf_op jit(solution)/shard_map/ppermute | solution.py:289
  126.2 4.6 %collective-permute-start.11 = (f32[32,128]{1,0:T(8,128)S(1)}, f32[32,128]{1,0:T(8,128)S(1)}, u32[]{:S(2)}, u32[]{:S(2)}) collective-permute-start(f32[32,128]{1,0:T(8,128)S(1)} %get-tuple-element.51.a_ref), channel_id=1, source_target_pairs={{0,2},{1,3},{2,0},{3,1},{4,6},{5,7},{6,4},{7,5},{8,10},{9,11},{10,... | collective-permute-start | bytes 49160 | tf_op jit(solution)/shard_map/ppermute | solution.py:289
  129.6 2.6 %collective-permute-start.12 = (f32[32,128]{1,0:T(8,128)S(1)}, f32[32,128]{1,0:T(8,128)S(1)}, u32[]{:S(2)}, u32[]{:S(2)}) collective-permute-start(f32[32,128]{1,0:T(8,128)S(1)} %get-tuple-element.52), channel_id=1, source_target_pairs={{0,3},{1,0},{2,1},{3,2},{4,7},{5,4},{6,5},{7,6},{8,11},{9,8},{10,9... | collective-permute-start | bytes 49160 | tf_op jit(solution)/shard_map/ppermute | solution.py:289
